TPU v7x, 128 devices: a whole 4x4x4 slice. The times are simulated.
128 devices in a mesh: space: 32 (over y, z, core), dp: 4 (over x).
Axes of the slice: x: 4, y: 4, z: 4, core: 2. Of those that a mesh axis runs over, the one named last changes fastest.
Arguments:
- forcing: bfloat16 [4, 512, 16, 8, 128], P('dp', 'space'), may hold values from -6 to 6
- hidden_prev: bfloat16 [4, 512, 64, 8, 128], P('dp', 'space'), may hold values from -0.8984375 to 0.8984375
- cell_prev: bfloat16 [4, 512, 64, 8, 128], P('dp', 'space'), may hold values from -4 to 4
- hidden_grad: bfloat16 [4, 512, 64, 8, 128], P('dp', 'space'), may hold values from -0.03125 to 0.03125
- w_gates: bfloat16 [256, 720], replicated, may hold values from -0.21875 to 0.21875
- gate_bias: float32 [256], replicated, may hold values from -4 to 4
- worker: int32 [4, 512], P('dp'), may hold values from -1 to 31, as said below
Outputs:
- hidden_next: bfloat16 [4, 512, 64, 8, 128], P('dp', 'space')
- cell_next: bfloat16 [4, 512, 64, 8, 128], P('dp', 'space')
- weight_grad: float32 [256, 720], P('space')
- bias_grad: float32 [256], P('space')
Inputs may be any that keep to these rules, and one draw needn't show every extreme that they name: Each year's active tiles (worker >= 0) are dealt to workers in increasing tile order: the j-th active tile, from 0, goes to worker j modulo the number of devices along space; every year has exactly 8 active tiles for every worker, one home in every year has all 16 of its tiles active, and so at most 1 tiles, reached, go from one home to one worker.
All inputs are finite; a program needn't handle non-finite values.
Results may differ from a plain program's by a relative error of at most 0.0075.
Values may be sent and summed in bfloat16 or wider, within the bound.
No kernel may reach another device: no remote copies, remote signals or barrier semaphores. Data moves between devices by JAX's collectives and lax.ppermute only.
A program may use at most 64 MiB of HBM per device.

v0:
```python
import jax
import jax.numpy as jnp
from jax import lax
from jax.sharding import PartitionSpec as P

TW = 4
BAND = 4


def extended(array, sides, width):
    for axis, dim in sides:
        size, length = (lax.axis_size(axis), array.shape[dim])
        up = [(i, (i + 1) % size) for i in range(size - 1)]
        down = [(j, i) for i, j in up]
        last = lax.slice_in_dim(array, length - width, length, axis=dim)
        leading = lax.slice_in_dim(array, 0, width, axis=dim)
        before = lax.ppermute(last, axis, up)
        after = lax.ppermute(leading, axis, down)
        array = jnp.concatenate([before, array, after], axis=dim)
    return array


def tile_step(window, cell_old, out_grad, flag, w_gates, gate_bias):
    in_width, rows_pad, cols_pad = window.shape
    tile_rows = rows_pad - 2
    tile_cols = cols_pad - 2
    hidden_width = cell_old.shape[0]
    cells = tile_rows * tile_cols
    patches = jnp.concatenate(
        [
            window[:, row_off : row_off + tile_rows, col_off : col_off + tile_cols].reshape(
                in_width, cells
            )
            for row_off in range(3)
            for col_off in range(3)
        ],
        axis=0,
    )
    pre = jnp.dot(w_gates, patches, preferred_element_type=jnp.float32) + gate_bias[:, None]
    pre = pre.reshape(4, hidden_width, cells)
    in_gate = jax.nn.sigmoid(pre[0])
    forget_gate = jax.nn.sigmoid(pre[1])
    out_gate = jax.nn.sigmoid(pre[2])
    candidate = jnp.tanh(pre[3])
    cell_before = cell_old.reshape(hidden_width, cells).astype(jnp.float32)
    cell_full = forget_gate * cell_before + in_gate * candidate
    squashed = jnp.tanh(cell_full)
    hidden_full = out_gate * squashed
    upstream = out_grad.reshape(hidden_width, cells).astype(jnp.float32)
    d_cell = upstream * out_gate * (1.0 - squashed * squashed)
    gate_grad = jnp.concatenate(
        [
            d_cell * candidate * in_gate * (1.0 - in_gate),
            d_cell * cell_before * forget_gate * (1.0 - forget_gate),
            upstream * squashed * out_gate * (1.0 - out_gate),
            d_cell * in_gate * (1.0 - candidate * candidate),
        ],
        axis=0,
    )
    gate_grad = (gate_grad * flag).astype(jnp.bfloat16)
    weight_part = lax.dot_general(
        gate_grad, patches, (((1,), (1,)), ((), ())), preferred_element_type=jnp.float32
    )
    bias_part = jnp.sum(gate_grad.astype(jnp.float32), axis=1)
    hidden_new = hidden_full.astype(jnp.bfloat16).reshape(hidden_width, tile_rows, tile_cols)
    cell_new = cell_full.astype(jnp.bfloat16).reshape(hidden_width, tile_rows, tile_cols)
    return (hidden_new, cell_new, weight_part, bias_part)


def run_tiles(windows, cell_olds, out_grads, flags, w_gates, gate_bias, grad_init):

    def one_tile(carry, item):
        window, cell_old, out_grad, flag = item
        hidden_new, cell_new, weight_part, bias_part = tile_step(
            window, cell_old, out_grad, flag, w_gates, gate_bias
        )
        return ((carry[0] + weight_part, carry[1] + bias_part), (hidden_new, cell_new))

    return lax.scan(one_tile, grad_init, (windows, cell_olds, out_grads, flags))


def shards(forcing, hidden_prev, cell_prev, hidden_grad, w_gates, gate_bias, worker):
    years, tiles_home, in_ch, tile_rows, tile_cols = forcing.shape
    hidden_width = hidden_prev.shape[2]
    in_width = in_ch + hidden_width
    gate_count = w_gates.shape[0]
    devices = lax.axis_size("space")
    my_index = lax.axis_index("space")
    grad_state = (jnp.zeros(w_gates.shape, jnp.float32), jnp.zeros(gate_bias.shape, jnp.float32))
    whole = worker[0]
    mine = lax.dynamic_slice_in_dim(whole, my_index * tiles_home, tiles_home)
    my_live = mine >= 0
    joined = jnp.concatenate([forcing[0], hidden_prev[0]], axis=1)
    band = joined.reshape(BAND, TW, in_width, tile_rows, tile_cols).transpose(2, 0, 3, 1, 4)
    band = band.reshape(in_width, BAND * tile_rows, TW * tile_cols)
    grown = extended(band, (("space", 1),), 1)
    grown = jnp.pad(grown, ((0, 0), (0, 0), (1, 1)))
    windows = jnp.stack(
        [
            grown[
                :,
                block_row * tile_rows : block_row * tile_rows + tile_rows + 2,
                block_col * tile_cols : block_col * tile_cols + tile_cols + 2,
            ]
            for block_row in range(BAND)
            for block_col in range(TW)
        ]
    )
    flags = my_live.astype(jnp.float32)
    grad_state, (hidden_done, cell_done) = run_tiles(
        windows, cell_prev[0], hidden_grad[0], flags, w_gates, gate_bias, grad_state
    )
    live_mask = my_live[:, None, None, None]
    hidden_list = [jnp.where(live_mask, hidden_done, hidden_prev[0])]
    cell_list = [jnp.where(live_mask, cell_done, cell_prev[0])]
    grad_weights, grad_bias = grad_state
    total_weights, total_bias = lax.psum((grad_weights, grad_bias), ("space", "dp"))
    share = gate_count // devices
    out_weights = lax.dynamic_slice_in_dim(total_weights, my_index * share, share, 0)
    out_bias = lax.dynamic_slice_in_dim(total_bias, my_index * share, share, 0)
    return (jnp.stack(hidden_list), jnp.stack(cell_list), out_weights, out_bias)


def solution(mesh):
    placed = (
        P("dp", "space", None, None, None),
        P("dp", "space", None, None, None),
        P("dp", "space", None, None, None),
        P("dp", "space", None, None, None),
        P(),
        P(),
        P("dp", None),
    )
    return jax.shard_map(
        shards,
        mesh=mesh,
        in_specs=placed,
        out_specs=(
            P("dp", "space", None, None, None),
            P("dp", "space", None, None, None),
            P("space", None),
            P("space"),
        ),
        check_vma=False,
    )
```

profile of v0, /device:TPU:0, one launch (start us, length us, event | category | flops | bytes accessed | tf_op | source)
XLA Modules:
  0.0 327.5 jit_solution(15897453523664863339)
XLA Ops:
  7.2 2.1 copy_bitcast_fusion
  12.9 3.5 %collective-permute-done.1 = bf16[80,1,512]{2,1,0:T(2,128)(2,1)S(1)} collective-permute-done((bf16[80,1,512]{2,1,0:T(2,128)(2,1)S(1)}, bf16[80,1,512]{2,1,0:T(2,128)(2,1)S(1)}, u32[]{:S(2)}, u32[]{:S(2)}) %collective-permute-start.1) | collective-permute-done | bytes 81952 | tf_op jit(solution)/shard_map/ppermute | solution.py:18
  16.4 4.4 %fusion.30 = bf16[80,34,514]{2,1,0:T(8,128)(2,1)S(1)} fusion(bf16[80,1,512]{2,1,0:T(2,128)(2,1)S(1)} %collective-permute-done.1, bf16[80,32,512]{2,1,0:T(8,128)(2,1)S(1)} %copy_bitcast_fusion, bf16[80,1,512]{2,1,0:T(2,128)(2,1)S(1)} %collective-permute-done), kind=kLoop, calls=%fused_computation.62 | loop fusion | flops 16776960 | bytes 5581440 | tf_op jit(solution)/shard_map/concatenate | solution.py:19
  26.9 4.0 %copy-done.1 = bf16[16,80,10,130]{3,2,1,0:T(8,128)(2,1)} copy-done((bf16[16,80,10,130]{3,2,1,0:T(8,128)(2,1)}, bf16[16,80,10,130]{3,2,1,0:T(8,128)(2,1)S(1)}, u32[]{:S(2)}) %copy-start.1) | copy-done | bytes 3328024
  30.8 133.0 %while.17 = (s32[]{:T(128)}, f32[256,720]{0,1:T(8,128)S(1)}, f32[256]{0:T(256)S(1)}, bf16[16,64,8,128]{3,2,1,0:T(8,128)(2,1)}, bf16[16,64,8,128]{3,2,1,0:T(8,128...) while((s32[]{:T(128)}, f32[256,720]{0,1:T(8,128)S(1)}, ...), condition=%wide.region_2.3_spmd.clone, body=%wide.region_0.2_spmd.clone.sunk | while | flops 762552576 | bytes 26218424 | solution.py:79
  34.0 1.7 convert_dynamic-update-slice_fusion.2
  42.3 1.7 convert_dynamic-update-slice_fusion.2
  50.6 1.7 convert_dynamic-update-slice_fusion.2
  58.9 1.7 convert_dynamic-update-slice_fusion.2
  67.3 1.7 convert_dynamic-update-slice_fusion.2
  75.6 1.7 convert_dynamic-update-slice_fusion.2
  83.9 1.7 convert_dynamic-update-slice_fusion.2
  92.2 1.7 convert_dynamic-update-slice_fusion.2
  100.5 1.7 convert_dynamic-update-slice_fusion.2
  108.8 1.7 convert_dynamic-update-slice_fusion.2
  117.1 1.7 convert_dynamic-update-slice_fusion.2
  125.4 1.7 convert_dynamic-update-slice_fusion.2
  133.8 1.7 convert_dynamic-update-slice_fusion.2
  142.1 1.7 convert_dynamic-update-slice_fusion.2
  150.4 1.7 convert_dynamic-update-slice_fusion.2
  158.7 1.7 convert_dynamic-update-slice_fusion.2
  165.0 71.2 %psum.15 = f32[256]{0:T(256)S(1)} all-reduce(f32[256]{0:T(256)S(1)} %get-tuple-element.67), channel_id=1, replica_groups=mesh['space'=32,'dp'=4] {'space','dp'}, use_global_device_ids=true, to_apply=%region_4.5 | all-reduce | flops 256 | bytes 2048 | tf_op jit(solution)/shard_map/psum | solution.py:117
  236.8 5.4 %select_bitcast_fusion = (bf16[1,16,64,8,128]{4,3,2,1,0:T(8,128)(2,1)}, bf16[1,16,64,8,128]{4,3,2,1,0:T(8,128)(2,1)}) fusion(bf16[16,64,8,128]{3,2,1,0:T(8,128)(2,1)} %get-tuple-element.65, pred[16]{0:T(512)(128)(4,1)S(1)} %get-tuple-element.130, bf16[1,16,64,8,128]{4,3,2,1,0:T(8,128)(2,1)} %bitcast.254, bf16[16,64,8,128]{3,2,1,0:T(8,128)(2,1)} %get-tuple-element.64, ...), kind=kLoop, calls=%fused_computation.67 | loop fusion | flops 2097152 | bytes 12582928 | tf_op jit(solution)/shard_map/stack | solution.py:121
  242.2 77.1 %all-reduce.3.cloned.1.call-done = f32[256,720]{1,0:T(8,128)} async-done(((f32[256,720]{1,0:T(8,128)}), f32[256,720]{1,0:T(8,128)}) %all-reduce.3.cloned.1.call-update) | async-done | bytes 737296 | tf_op jit(solution)/shard_map/psum | solution.py:117
  (421 shorter events, 115.3 us)
Async XLA Ops:
  7.2 312.1 %all-reduce.3.cloned.1.call-start = ((), (), s32[]{:S(2)}) async-start(), calls=%async_computation | async-start | bytes 1572864 | tf_op jit(solution)/shard_map/psum | solution.py:117
  9.5 3.4 %collective-permute-start = (bf16[80,1,512]{2,1,0:T(2,128)(2,1)S(1)}, bf16[80,1,512]{2,1,0:T(2,128)(2,1)S(1)}, u32[]{:S(2)}, u32[]{:S(2)}) collective-permute-start(bf16[80,1,512]{2,1,0:T(2,128)(2,1)S(1)} %get-tuple-element.150), channel_id=1, source_target_pairs={{0,4},{4,8},{8,12},{12,16},{16,20},{20,24},{24,28},{28,32},{32,36}... | collective-permute-start | bytes 245768 | tf_op jit(solution)/shard_map/ppermute | solution.py:17
  10.8 5.5 %collective-permute-start.1 = (bf16[80,1,512]{2,1,0:T(2,128)(2,1)S(1)}, bf16[80,1,512]{2,1,0:T(2,128)(2,1)S(1)}, u32[]{:S(2)}, u32[]{:S(2)}) collective-permute-start(bf16[80,1,512]{2,1,0:T(2,128)(2,1)S(1)} %get-tuple-element.151), channel_id=1, source_target_pairs={{4,0},{8,4},{12,8},{16,12},{20,16},{24,20},{28,24},{32,28},{36,32}... | collective-permute-start | bytes 245768 | tf_op jit(solution)/shard_map/ppermute | solution.py:18
  26.0 4.8 %copy-start.2 = (f32[256,720]{0,1:T(8,128)S(1)}, f32[256,720]{0,1:T(8,128)}, u32[]{:S(2)}) copy-start(f32[256,720]{0,1:T(8,128)} %custom-call) | copy-start | bytes 2211844
  26.0 4.8 %copy-start.4 = (f32[256]{0:T(256)S(1)}, f32[256]{0:T(256)}, u32[]{:S(2)}) copy-start(f32[256]{0:T(256)} %param.14) | copy-start | bytes 3076
  26.9 4.0 %copy-start.1 = (bf16[16,80,10,130]{3,2,1,0:T(8,128)(2,1)}, bf16[16,80,10,130]{3,2,1,0:T(8,128)(2,1)S(1)}, u32[]{:S(2)}) copy-start(bf16[16,80,10,130]{3,2,1,0:T(8,128)(2,1)S(1)} %fusion.32) | copy-start | bytes 9984004
  32.0 1.0 copy-start.3
  40.3 1.0 copy-start.3
  48.6 1.0 copy-start.3
  56.9 1.0 copy-start.3
  65.2 1.0 copy-start.3
  73.5 1.0 copy-start.3
  81.8 1.0 copy-start.3
  90.1 1.0 copy-start.3
  98.5 1.0 copy-start.3
  106.8 1.0 copy-start.3
  115.1 1.0 copy-start.3
  123.4 1.0 copy-start.3
  131.7 1.0 copy-start.3
  140.0 1.0 copy-start.3
  148.3 1.0 copy-start.3
  156.6 1.0 copy-start.3
  163.8 73.0 %copy-start = (bf16[1,16,64,8,128]{4,3,2,1,0:T(8,128)(2,1)S(1)}, bf16[1,16,64,8,128]{4,3,2,1,0:T(8,128)(2,1)}, u32[]{:S(2)}) copy-start(bf16[1,16,64,8,128]{4,3,2,1,0:T(8,128)(2,1)} %param.10) | copy-start | bytes 6291460
Sparse Core Ops, SparseCore 0:
  165.1 154.1 all-reduce.2
where the time goes:
time: 330 us; the launch traced here: 327 us
  waiting for transfers between devices  80.6 us (24%)
  blocking collectives  71.2 us (22%)
  other arithmetic  70.1 us (21%)
  local copies, waits for them, and re-layouts  54.6 us (17%)
  matrix products  31.6 us (10%)
  between operations  14.2 us (4%)
    psum x1, waiting for transfers between devices, shards(): lax.psum((grad_weights, grad_bias), ('space', 'dp'))  77.1 us
    psum x1, blocking collectives, shards(): lax.psum((grad_weights, grad_bias), ('space', 'dp'))  71.2 us
    dynamic_update_slice x16, other arithmetic, run_tiles(): return lax.scan(one_tile, grad_init, (windows, cell_olds, out_grads, flags))  27.9 us
    dot_general x16, matrix products, tile_step(): lax.dot_general(gate_grad, patches, (((1,), (1,)), ((), ())), preferred_e...  21.5 us
    squeeze x16, local copies, waits for them, and re-layouts, run_tiles(): return lax.scan(one_tile, grad_init, (windows, cell_olds, out_grads, flags))  18.1 us
    reduce_sum x16, other arithmetic, tile_step(): bias_part = jnp.sum(gate_grad.astype(jnp.float32), axis=1)  12.7 us
    dot_general x16, matrix products, tile_step(): jnp.dot(w_gates, patches, preferred_element_type=jnp.float32)  10.1 us
    dynamic_slice x16, local copies, waits for them, and re-layouts, run_tiles(): return lax.scan(one_tile, grad_init, (windows, cell_olds, out_grads, flags))  9.42 us
  transfers between devices with their start and end apart: 3, of which 2 were waited for; matrix products, arithmetic and copies ran while one was open for 2% of the time, Pallas kernels for 0%

commit v1 on v0

v1 whole, which is shorter than its diff:
```python
import functools

import jax
import jax.numpy as jnp
from jax import lax
from jax.experimental import pallas as pl
from jax.experimental.pallas import tpu as pltpu
from jax.sharding import PartitionSpec as P

CIN = 16
HID = 64
KIN = CIN + HID
GATES = 4 * HID
ROWS = 8
COLS = 128
TW = 4
BAND = 4
WIDE = 3 * KIN
TAPS = 3 * WIDE
DEEP = 768
TALL = TAPS + 16

F32 = jnp.float32
BF16 = jnp.bfloat16


def load_rows(stage, tile, row, count):
    return stage[tile, pl.ds(row, count, stride=ROWS), :]


def build_row(patch_ref, line, pieces, lane):
    zero = jnp.zeros((KIN, COLS), F32)
    right = [pltpu.roll(piece, 1, 1) for piece in pieces]
    left = [pltpu.roll(piece, COLS - 1, 1) for piece in pieces]
    for tile in range(TW):
        before = right[tile - 1] if tile else zero
        after = left[tile + 1] if tile < TW - 1 else zero
        shifted = (
            jnp.where(lane == 0, before, right[tile]),
            pieces[tile],
            jnp.where(lane == COLS - 1, after, left[tile]),
        )
        span = slice(tile * COLS, (tile + 1) * COLS)
        for offset, value in enumerate(shifted):
            patch_ref[pl.ds(line * WIDE + offset * KIN, KIN), span] = value.astype(BF16)


def compute_kernel(
    first, step, last,
    worker_ref, forcing_ref, hidden_ref, cell_ref, grad_ref, above_ref, below_ref, weight_ref, bias_ref,
    *rest,
):
    if last:
        acc_in_ref, _, _, hidden_out, cell_out, sum_out = rest[:6]
        scratch = rest[6:]
    else:
        hidden_out, cell_out, sum_out = rest[:3]
        scratch = rest[3:]
    patch_ref, joined_ref, before_ref, up_ref, hidden_new, cell_new, w_ref, bias_b, total_ref = scratch
    part = pl.program_id(0)
    home = lax.axis_index("space")
    band_row = first + part * step
    base = home * (BAND * TW) + band_row * TW

    @pl.when(part == 0)
    def _():
        w_ref[...] = jnp.zeros((GATES, DEEP), BF16)
        scale = jnp.where(lax.broadcasted_iota(jnp.int32, (GATES, 1), 0) < 3 * HID, 0.5, 1.0).astype(F32)
        w_ref[:, :TAPS] = (weight_ref[...].astype(F32).T * scale).astype(BF16)
        bias_b[...] = jnp.broadcast_to(bias_ref[...] * scale, (GATES, COLS))
        patch_ref[(ROWS + 2) * WIDE :, :] = jnp.zeros((DEEP - TAPS, TW * COLS), BF16)
        if last:
            total_ref[...] = acc_in_ref[...]
        else:
            total_ref[...] = jnp.zeros_like(total_ref)

    lane = lax.broadcasted_iota(jnp.int32, (KIN, COLS), 1)
    for tile in range(TW):
        joined_ref[tile, : CIN * ROWS, :] = forcing_ref[tile].astype(F32).reshape(CIN * ROWS, COLS)
        joined_ref[tile, CIN * ROWS :, :] = hidden_ref[tile].astype(F32).reshape(HID * ROWS, COLS)
        before_ref[tile] = cell_ref[tile].astype(F32).reshape(HID * ROWS, COLS)
        live = worker_ref[base + tile] >= 0
        up = grad_ref[tile].astype(F32).reshape(HID * ROWS, COLS)
        up_ref[tile] = jnp.where(live, up, 0.0)

    build_row(patch_ref, 0, [above_ref[0, tile].astype(F32) for tile in range(TW)], lane)
    build_row(patch_ref, ROWS + 1, [below_ref[0, tile].astype(F32) for tile in range(TW)], lane)
    for row in range(ROWS):
        build_row(patch_ref, row + 1, [load_rows(joined_ref, tile, row, KIN) for tile in range(TW)], lane)

    ones = jnp.ones((TALL - TAPS, TW * COLS), BF16)

    def one_row(row, carry):
        at = pl.multiple_of(row * WIDE, 16)
        pre = jnp.dot(w_ref[...], patch_ref[pl.ds(at, DEEP), :], preferred_element_type=F32)
        grads = []
        for tile in range(TW):
            span = slice(tile * COLS, (tile + 1) * COLS)
            blocks = [
                jnp.tanh(pre[k * HID : (k + 1) * HID, span] + bias_b[k * HID : (k + 1) * HID, :]) for k in range(4)
            ]
            in_gate, forget_gate, out_gate = [0.5 * block + 0.5 for block in blocks[:3]]
            candidate = blocks[3]
            cell_before = load_rows(before_ref, tile, row, HID)
            upstream = load_rows(up_ref, tile, row, HID)
            cell_full = forget_gate * cell_before + in_gate * candidate
            squashed = jnp.tanh(cell_full)
            hidden_new[tile, pl.ds(row, HID, stride=ROWS), :] = out_gate * squashed
            cell_new[tile, pl.ds(row, HID, stride=ROWS), :] = cell_full
            raised = upstream * out_gate
            d_cell = raised * (1.0 - squashed * squashed)
            d_in = d_cell * in_gate
            grads.append(
                jnp.concatenate(
                    [
                        d_in * candidate * (1.0 - in_gate),
                        d_cell * cell_before * forget_gate * (1.0 - forget_gate),
                        raised * squashed * (1.0 - out_gate),
                        d_in * (1.0 - candidate * candidate),
                    ],
                    axis=0,
                ).astype(BF16)
            )
        gate_grad = jnp.concatenate(grads, axis=1)
        left = jnp.concatenate([patch_ref[pl.ds(at, TAPS), :], ones], axis=0)
        total_ref[...] += lax.dot_general(
            left, gate_grad, (((1,), (1,)), ((), ())), preferred_element_type=F32
        )
        return carry

    lax.fori_loop(0, ROWS, one_row, 0)

    for tile in range(TW):
        live = worker_ref[base + tile] >= 0
        fresh = hidden_new[tile].reshape(HID, ROWS, COLS).astype(BF16)
        hidden_out[tile] = jnp.where(live, fresh, hidden_ref[tile])
        fresh = cell_new[tile].reshape(HID, ROWS, COLS).astype(BF16)
        cell_out[tile] = jnp.where(live, fresh, cell_ref[tile])

    @pl.when(part == 1)
    def _():
        if last:
            sum_out[:, :TALL] = total_ref[...].T.astype(BF16)
            sum_out[:, TALL:] = jnp.zeros((GATES, DEEP - TALL), BF16)
        else:
            sum_out[...] = total_ref[...]


def compute(first, step, worker, forcing, hidden, cell, grad, above, below, weight, bias, carried=None):
    last = carried is not None

    def block(channels):
        return pl.BlockSpec((TW, channels, ROWS, COLS), lambda part, _: (first + part * step, 0, 0, 0))

    edge = pl.BlockSpec((1, TW, KIN, COLS), lambda part, _: (part, 0, 0, 0))

    def whole(*shape):
        return pl.BlockSpec(shape, lambda part, _: (0,) * len(shape), pipeline_mode=pl.Buffered(1))

    in_specs = [block(CIN), block(HID), block(HID), block(HID), edge, edge, whole(TAPS, GATES), whole(GATES, 1)]
    operands = [worker, forcing, hidden, cell, grad, above, below, weight, bias]
    aliases = {}
    if last:
        in_specs += [whole(TALL, GATES), pl.BlockSpec(memory_space=pl.ANY), pl.BlockSpec(memory_space=pl.ANY)]
        aliases = {len(operands) + 1: 0, len(operands) + 2: 1}
        operands += list(carried)
        sum_shape = jax.ShapeDtypeStruct((GATES, DEEP), BF16)
    else:
        sum_shape = jax.ShapeDtypeStruct((TALL, GATES), F32)
    state = jax.ShapeDtypeStruct(hidden.shape, BF16)
    stage = pltpu.VMEM((TW, HID * ROWS, COLS), F32)
    return pl.pallas_call(
        functools.partial(compute_kernel, first, step, last),
        grid_spec=pltpu.PrefetchScalarGridSpec(
            num_scalar_prefetch=1,
            grid=(2,),
            in_specs=in_specs,
            out_specs=[block(HID), block(HID), whole(*sum_shape.shape)],
            scratch_shapes=[
                pltpu.VMEM(((ROWS + 2) * WIDE + DEEP - TAPS, TW * COLS), BF16),
                pltpu.VMEM((TW, KIN * ROWS, COLS), F32),
                stage, stage, stage, stage,
                pltpu.VMEM((GATES, DEEP), BF16),
                pltpu.VMEM((GATES, COLS), F32),
                pltpu.VMEM((TALL, GATES), F32),
            ],
        ),
        out_shape=[state, state, sum_shape],
        input_output_aliases=aliases,
        compiler_params=pltpu.CompilerParams(vmem_limit_bytes=40 << 20),
        cost_estimate=pl.CostEstimate(
            flops=8 * TW * ROWS * COLS * TAPS * GATES, bytes_accessed=6 << 20, transcendentals=0
        ),
        name="second" if last else "first",
    )(*operands)


def shards(forcing, hidden_prev, cell_prev, hidden_grad, w_gates, gate_bias, worker):
    size = lax.axis_size("space")
    forcing, hidden, cell, grad = forcing[0], hidden_prev[0], cell_prev[0], hidden_grad[0]
    joined_f = forcing.reshape(BAND, TW, CIN, ROWS, COLS)
    joined_h = hidden.reshape(BAND, TW, HID, ROWS, COLS)
    leading = jnp.concatenate([joined_f[:, :, :, 0], joined_h[:, :, :, 0]], axis=2)
    ending = jnp.concatenate([joined_f[:, :, :, ROWS - 1], joined_h[:, :, :, ROWS - 1]], axis=2)
    up = [(i, i + 1) for i in range(size - 1)]
    down = [(j, i) for i, j in up]
    before = lax.ppermute(ending[BAND - 1 :], "space", up)
    after = lax.ppermute(leading[:1], "space", down)
    weight = w_gates.T
    bias = gate_bias[:, None]
    tiles = worker[0]
    carried = compute(
        1, 1, tiles, forcing, hidden, cell, grad, ending[0:2], leading[2:4], weight, bias
    )
    above = jnp.concatenate([before, ending[2:3]], axis=0)
    below = jnp.concatenate([leading[1:2], after], axis=0)
    hidden_next, cell_next, part = compute(
        0, 3, tiles, forcing, hidden, cell, grad, above, below, weight, bias,
        carried=(carried[2], carried[0], carried[1]),
    )
    share = GATES // size
    pieces = lax.all_to_all(part.reshape(size, share, DEEP), "space", 0, 0, tiled=True)
    mine = jnp.sum(pieces.astype(F32), axis=0).astype(BF16)
    years = lax.axis_size("dp")
    total = mine.astype(F32)
    for k in range(1, years):
        other = lax.ppermute(mine, "dp", [(i, (i + k) % years) for i in range(years)])
        total = total + other.astype(F32)
    return hidden_next[None], cell_next[None], total[:, :TAPS], total[:, TAPS]


def solution(mesh):
    tiles = P("dp", "space", None, None, None)
    return jax.shard_map(
        shards,
        mesh=mesh,
        in_specs=(tiles, tiles, tiles, tiles, P(), P(), P("dp", None)),
        out_specs=(tiles, tiles, P("space", None), P("space")),
        check_vma=False,
    )
```

time: 330 us -> 83.4 us (0.25)
  waiting for transfers between devices: 80.6 us -> 6.67 us
  other arithmetic: 70.1 us -> 3.32 us
  blocking collectives: 71.2 us -> 20.9 us
  local copies, waits for them, and re-layouts: 54.6 us -> 7.35 us
  Pallas kernels: 0 us -> 36.1 us
  matrix products: 31.6 us -> 0 us
  between operations: 14.2 us -> 0.81 us
  starting transfers between devices: 2.63 us -> 7.82 us
    psum x1 -> x0, waiting for transfers between devices: 77.1 us -> none  [shards(): lax.psum((grad_weights, grad_bias), ('space', 'dp'))]
    psum x1 -> x0, blocking collectives: 71.2 us -> none  [shards(): lax.psum((grad_weights, grad_bias), ('space', 'dp'))]
    pallas_call x0 -> x2, Pallas kernels: none -> 36.1 us  [compute(): pl.pallas_call(functools.partial(compute_kernel, first, step, last), grid...]
    dot_general x32 -> x0, matrix products: 31.6 us -> none  [the longest x16 21.5 us: tile_step(): lax.dot_general(gate_grad, patches, (((1,), (1,)), ((), ())), preferred_e...]
    dynamic_update_slice x16 -> x0, other arithmetic: 27.9 us -> none  [run_tiles(): return lax.scan(one_tile, grad_init, (windows, cell_olds, out_grads, flags))]
    all_to_all x0 -> x1, blocking collectives: none -> 20.9 us  [shards(): lax.all_to_all(part.reshape(size, share, DEEP), 'space', 0, 0, tiled=True)]
    squeeze x16 -> x2, local copies, waits for them, and re-layouts: 18.1 us -> 0.05 us  [the longest x1 0.04 us: shards(): joined_h[:, :, :, 0]]
    reduce_sum x16 -> x1, other arithmetic: 12.7 us -> 0.07 us  [shards(): mine = jnp.sum(pieces.astype(F32), axis=0).astype(BF16)]
  transfers between devices with their start and end apart: 3 -> 5, of which waited for: 2 -> 3; matrix products, arithmetic and copies ran while one was open for 2% -> 2% of each run, Pallas kernels for 0% -> 0%
where the time goes in v1:
time: 83.4 us; the launch traced here: 83 us
  Pallas kernels  36.1 us (43%)
  blocking collectives  20.9 us (25%)
  starting transfers between devices  7.82 us (9%)
  local copies, waits for them, and re-layouts  7.35 us (9%)
  waiting for transfers between devices  6.67 us (8%)
  other arithmetic  3.32 us (4%)
    pallas_call x2, Pallas kernels, compute(): pl.pallas_call(functools.partial(compute_kernel, first, step, last), grid...  36.1 us
    all_to_all x1, blocking collectives, shards(): lax.all_to_all(part.reshape(size, share, DEEP), 'space', 0, 0, tiled=True)  20.9 us
    unnamed x20, local copies, waits for them, and re-layouts  6.47 us
    ppermute x3, starting transfers between devices, shards(): lax.ppermute(mine, 'dp', [(i, (i + k) % years) for i in range(years)])  4.51 us
    ppermute x3, waiting for transfers between devices, shards(): lax.ppermute(mine, 'dp', [(i, (i + k) % years) for i in range(years)])  4.02 us
    ppermute x1, waiting for transfers between devices, shards(): after = lax.ppermute(leading[:1], 'space', down)  2.65 us
    ppermute x1, starting transfers between devices, shards(): before = lax.ppermute(ending[BAND - 1:], 'space', up)  2.03 us
  transfers between devices with their start and end apart: 5, of which 3 were waited for; matrix products, arithmetic and copies ran while one was open for 2% of the time, Pallas kernels for 0%

profile of v1, /device:TPU:0, one launch (start us, length us, event | category | flops | bytes accessed | tf_op | source)
XLA Modules:
  0.0 83.0 jit_solution(1224988211373918674)
XLA Ops:
  0.6 1.1 %copy.15 = bf16[1,16,16,8,128]{4,2,1,3,0:T(8,128)(2,1)S(1)} copy(bf16[1,16,16,8,128]{4,3,2,1,0:T(8,128)(2,1)} %param.7) | data formatting | bytes 1048576 | tf_op args[0]
  1.8 0.0 copy-start.8
  1.8 2.1 %copy.16 = bf16[1,16,64,8,128]{4,2,1,3,0:T(8,128)(2,1)S(1)} copy(bf16[1,16,64,8,128]{4,3,2,1,0:T(8,128)(2,1)} %param.8) | data formatting | bytes 4194304 | tf_op args[1]
  4.0 0.6 pad_maximum_fusion.3
  4.7 2.0 %collective-permute-start = (bf16[1,4,80,128]{3,2,1,0:T(8,128)(2,1)}, bf16[1,4,80,128]{3,2,1,0:T(8,128)(2,1)}, u32[]{:S(2)}, u32[]{:S(2)}) collective-permute-start(bf16[1,4,80,128]{3,2,1,0:T(8,128)(2,1)} %pad_maximum_fusion.3), channel_id=1, source_target_pairs={{0,4},{4,8},{8,12},{12,16},{16,20},{20,24},{24,28},{28,32},{32,36}... | collective-permute-start | bytes 245768 | tf_op jit(solution)/shard_map/ppermute | solution.py:207
  6.7 0.6 pad_maximum_fusion.2
  7.3 1.3 %collective-permute-start.1 = (bf16[1,4,80,128]{3,2,1,0:T(8,128)(2,1)}, bf16[1,4,80,128]{3,2,1,0:T(8,128)(2,1)}, u32[]{:S(2)}, u32[]{:S(2)}) collective-permute-start(bf16[1,4,80,128]{3,2,1,0:T(8,128)(2,1)} %pad_maximum_fusion.2), channel_id=1, source_target_pairs={{4,0},{8,4},{12,8},{16,12},{20,16},{24,20},{28,24},{32,28},{36,32}... | collective-permute-start | bytes 245768 | tf_op jit(solution)/shard_map/ppermute | solution.py:208
  8.6 0.1 copy.18.bias_ref
  8.8 1.0 %pad_maximum_fusion.1 = (bf16[2,4,80,128]{3,2,1,0:T(8,128)(2,1)S(1)}, bf16[2,4,80,128]{3,2,1,0:T(8,128)(2,1)S(1)}) fusion(bf16[4,4,64,128]{3,2,1,0:T(8,128)(2,1)} %copy-done.6, bf16[4,4,16,128]{3,2,1,0:T(8,128)(2,1)S(1)} %get-tuple-element.19, bf16[1,4,80,128]{3,2,1,0:T(8,128)(2,1)} %collective-permute-done), kind=kLoop, calls=%fused_computation.13 | loop fusion | flops 1064960 | bytes 737280 | tf_op jit(solution)/shard_map/concatenate | solution.py:204
  9.8 2.6 %collective-permute-done.1 = bf16[1,4,80,128]{3,2,1,0:T(8,128)(2,1)} collective-permute-done((bf16[1,4,80,128]{3,2,1,0:T(8,128)(2,1)}, bf16[1,4,80,128]{3,2,1,0:T(8,128)(2,1)}, u32[]{:S(2)}, u32[]{:S(2)}) %collective-permute-start.1) | collective-permute-done | bytes 81952 | tf_op jit(solution)/shard_map/ppermute | solution.py:208
  12.5 0.9 %pad_maximum_fusion = (bf16[2,4,80,128]{3,2,1,0:T(8,128)(2,1)S(1)}, bf16[2,4,80,128]{3,2,1,0:T(8,128)(2,1)S(1)}) fusion(bf16[4,4,64,128]{3,2,1,0:T(8,128)(2,1)S(1)} %get-tuple-element.16, bf16[4,4,16,128]{3,2,1,0:T(8,128)(2,1)S(1)} %get-tuple-element.18, bf16[1,4,80,128]{3,2,1,0:T(8,128)(2,1)} %collective-permute-done.1), kind=kLoop, calls=%fused_computation.12 | loop fusion | flops 1064960 | bytes 737280 | tf_op jit(solution)/shard_map/concatenate | solution.py:203
  13.5 1.6 %copy-done.2 = bf16[1,16,64,8,128]{4,3,2,1,0:T(8,128)(2,1)S(1)} copy-done((bf16[1,16,64,8,128]{4,3,2,1,0:T(8,128)(2,1)S(1)}, bf16[1,16,64,8,128]{4,3,2,1,0:T(8,128)(2,1)}, u32[]{:S(2)}) %copy-start.2) | copy-done | bytes 2097176
  15.0 1.6 %copy-done.3 = bf16[1,16,64,8,128]{4,3,2,1,0:T(8,128)(2,1)S(1)} copy-done((bf16[1,16,64,8,128]{4,3,2,1,0:T(8,128)(2,1)S(1)}, bf16[1,16,64,8,128]{4,3,2,1,0:T(8,128)(2,1)}, u32[]{:S(2)}) %copy-start.3) | copy-done | bytes 2097176
  16.6 18.0 %first.1 = (bf16[16,64,8,128]{3,2,1,0:T(8,128)(2,1)}, bf16[16,64,8,128]{3,2,1,0:T(8,128)(2,1)}, f32[736,256]{1,0:T(8,128)S(1)}) custom-call(s32[512]{0:T(512)S(1)} %bitcast.32, bf16[16,16,8,128]{3,2,1,0:T(8,128)(2,1)S(1)} %bitcast.23, bf16[16,64,8,128]{3,2,1,0:T(8,128)(2,1)S(1)} %bitcast.21, bf16[16,64,8,128]{3,2,1,0:T(8,128)(2,1)S(1)} %bitcast.26, ...), custom_call_target="tpu_custom_call" | custom-call | flops 6039797760 | bytes 6291456 | tf_op jit(solution)/shard_map/first/pallas_call | solution.py:172
  34.6 18.1 %second.1 = (bf16[16,64,8,128]{3,2,1,0:T(8,128)(2,1)}, bf16[16,64,8,128]{3,2,1,0:T(8,128)(2,1)}, bf16[256,768]{1,0:T(8,128)(2,1)S(1)}) custom-call(s32[512]{0:T(512)S(1)} %bitcast.33, bf16[16,16,8,128]{3,2,1,0:T(8,128)(2,1)S(1)} %bitcast.24, bf16[16,64,8,128]{3,2,1,0:T(8,128)(2,1)S(1)} %bitcast.22, ...), custom_call_target="tpu_custom_call", output_to_operand_aliasing={{0}: (10, {}), {1}: (11, {})} | custom-call | flops 6039797760 | bytes 6291456 | tf_op jit(solution)/shard_map/second/pallas_call | solution.py:172
  52.8 20.9 %all_to_all.5 = bf16[32,8,768]{2,1,0:T(8,128)(2,1)S(1)} all-to-all(bf16[32,8,768]{2,1,0:T(8,128)(2,1)S(1)} %bitcast.25), channel_id=1, replica_groups=mesh['space'=32,'dp'=4] {'space'}, dimensions={0} | all-to-all | bytes 786432 | tf_op jit(solution)/shard_map/all_to_all | solution.py:222
  73.6 0.1 reduce_sum.12
  73.7 2.8 %collective-permute-start.4 = (bf16[8,768]{1,0:T(8,128)(2,1)S(1)}, bf16[8,768]{1,0:T(8,128)(2,1)S(1)}, u32[]{:S(2)}, u32[]{:S(2)}) collective-permute-start(bf16[8,768]{1,0:T(8,128)(2,1)S(1)} %reduce_sum.12), channel_id=1, source_target_pairs={{0,3},{1,0},{2,1},{3,2},{4,7},{5,4},{6,5},{7,6},{8,11},{9,8},{10,9... | collective-permute-start | bytes 36872 | tf_op jit(solution)/shard_map/ppermute | solution.py:227
  76.5 0.8 collective-permute-start.3
  77.3 0.9 %collective-permute-start.2 = (bf16[8,768]{1,0:T(8,128)(2,1)S(1)}, bf16[8,768]{1,0:T(8,128)(2,1)S(1)}, u32[]{:S(2)}, u32[]{:S(2)}) collective-permute-start(bf16[8,768]{1,0:T(8,128)(2,1)S(1)} %reduce_sum.12), channel_id=1, source_target_pairs={{0,1},{1,2},{2,3},{3,0},{4,5},{5,6},{6,7},{7,4},{8,9},{9,10},{10,1... | collective-permute-start | bytes 36872 | tf_op jit(solution)/shard_map/ppermute | solution.py:227
  78.2 3.5 %collective-permute-done.3 = bf16[8,768]{1,0:T(8,128)(2,1)S(1)} collective-permute-done((bf16[8,768]{1,0:T(8,128)(2,1)S(1)}, bf16[8,768]{1,0:T(8,128)(2,1)S(1)}, u32[]{:S(2)}, u32[]{:S(2)}) %collective-permute-start.3) | collective-permute-done | bytes 12320 | tf_op jit(solution)/shard_map/ppermute | solution.py:227
  81.7 0.5 collective-permute-done.2
  82.2 0.0 copy-start.7
  82.3 0.7 slice_reduce_fusion
  (19 shorter events, 0.1 us)
Async XLA Ops:
  1.8 6.9 %copy-start.8 = (f32[256]{0:T(256)S(1)}, f32[256]{0:T(256)}, u32[]{:S(2)}) copy-start(f32[256]{0:T(256)} %param.12) | copy-start | bytes 3076
  3.9 9.5 %copy-start = (bf16[1,16,64,8,128]{4,3,2,1,0:T(8,128)(2,1)S(1)}, bf16[1,16,64,8,128]{4,3,2,1,0:T(8,128)(2,1)}, u32[]{:S(2)}) copy-start(bf16[1,16,64,8,128]{4,3,2,1,0:T(8,128)(2,1)} %param.8) | copy-start | bytes 6291460
  3.9 9.5 %copy-start.1 = (bf16[1,16,16,8,128]{4,3,2,1,0:T(8,128)(2,1)S(1)}, bf16[1,16,16,8,128]{4,3,2,1,0:T(8,128)(2,1)}, u32[]{:S(2)}) copy-start(bf16[1,16,16,8,128]{4,3,2,1,0:T(8,128)(2,1)} %param.7) | copy-start | bytes 1572868
  3.9 9.5 %copy-start.4 = (bf16[256,720]{0,1:T(8,128)(2,1)S(1)}, bf16[256,720]{0,1:T(8,128)(2,1)}, u32[]{:S(2)}) copy-start(bf16[256,720]{0,1:T(8,128)(2,1)} %param.11) | copy-start | bytes 1105924
  4.0 9.5 %copy-start.5 = (s32[1,512]{1,0:T(1,128)S(1)}, s32[1,512]{1,0:T(1,128)}, u32[]{:S(2)}) copy-start(s32[1,512]{1,0:T(1,128)} %param.13) | copy-start | bytes 6148
  4.0 4.6 %copy-start.6 = (bf16[4,4,64,128]{3,2,1,0:T(8,128)(2,1)}, bf16[4,4,64,128]{3,2,1,0:T(8,128)(2,1)S(1)}, u32[]{:S(2)}) copy-start(bf16[4,4,64,128]{3,2,1,0:T(8,128)(2,1)S(1)} %get-tuple-element.17) | copy-start | bytes 786436
  4.7 4.1 %collective-permute-start = (bf16[1,4,80,128]{3,2,1,0:T(8,128)(2,1)}, bf16[1,4,80,128]{3,2,1,0:T(8,128)(2,1)}, u32[]{:S(2)}, u32[]{:S(2)}) collective-permute-start(bf16[1,4,80,128]{3,2,1,0:T(8,128)(2,1)} %pad_maximum_fusion.3), channel_id=1, source_target_pairs={{0,4},{4,8},{8,12},{12,16},{16,20},{20,24},{24,28},{28,32},{32,36}... | collective-permute-start | bytes 245768 | tf_op jit(solution)/shard_map/ppermute | solution.py:207
  7.3 5.2 %collective-permute-start.1 = (bf16[1,4,80,128]{3,2,1,0:T(8,128)(2,1)}, bf16[1,4,80,128]{3,2,1,0:T(8,128)(2,1)}, u32[]{:S(2)}, u32[]{:S(2)}) collective-permute-start(bf16[1,4,80,128]{3,2,1,0:T(8,128)(2,1)} %pad_maximum_fusion.2), channel_id=1, source_target_pairs={{4,0},{8,4},{12,8},{16,12},{20,16},{24,20},{28,24},{32,28},{36,32}... | collective-permute-start | bytes 245768 | tf_op jit(solution)/shard_map/ppermute | solution.py:208
  13.5 1.6 %copy-start.2 = (bf16[1,16,64,8,128]{4,3,2,1,0:T(8,128)(2,1)S(1)}, bf16[1,16,64,8,128]{4,3,2,1,0:T(8,128)(2,1)}, u32[]{:S(2)}) copy-start(bf16[1,16,64,8,128]{4,3,2,1,0:T(8,128)(2,1)} %param.9) | copy-start | bytes 6291460
  15.0 1.6 %copy-start.3 = (bf16[1,16,64,8,128]{4,3,2,1,0:T(8,128)(2,1)S(1)}, bf16[1,16,64,8,128]{4,3,2,1,0:T(8,128)(2,1)}, u32[]{:S(2)}) copy-start(bf16[1,16,64,8,128]{4,3,2,1,0:T(8,128)(2,1)} %param.10) | copy-start | bytes 6291460
  73.7 4.5 %collective-permute-start.4 = (bf16[8,768]{1,0:T(8,128)(2,1)S(1)}, bf16[8,768]{1,0:T(8,128)(2,1)S(1)}, u32[]{:S(2)}, u32[]{:S(2)}) collective-permute-start(bf16[8,768]{1,0:T(8,128)(2,1)S(1)} %reduce_sum.12), channel_id=1, source_target_pairs={{0,3},{1,0},{2,1},{3,2},{4,7},{5,4},{6,5},{7,6},{8,11},{9,8},{10,9... | collective-permute-start | bytes 36872 | tf_op jit(solution)/shard_map/ppermute | solution.py:227
  76.5 5.2 %collective-permute-start.3 = (bf16[8,768]{1,0:T(8,128)(2,1)S(1)}, bf16[8,768]{1,0:T(8,128)(2,1)S(1)}, u32[]{:S(2)}, u32[]{:S(2)}) collective-permute-start(bf16[8,768]{1,0:T(8,128)(2,1)S(1)} %reduce_sum.12), channel_id=1, source_target_pairs={{0,2},{1,3},{2,0},{3,1},{4,6},{5,7},{6,4},{7,5},{8,10},{9,11},{10,... | collective-permute-start | bytes 36872 | tf_op jit(solution)/shard_map/ppermute | solution.py:227
  77.3 4.9 %collective-permute-start.2 = (bf16[8,768]{1,0:T(8,128)(2,1)S(1)}, bf16[8,768]{1,0:T(8,128)(2,1)S(1)}, u32[]{:S(2)}, u32[]{:S(2)}) collective-permute-start(bf16[8,768]{1,0:T(8,128)(2,1)S(1)} %reduce_sum.12), channel_id=1, source_target_pairs={{0,1},{1,2},{2,3},{3,0},{4,5},{5,6},{6,7},{7,4},{8,9},{9,10},{10,1... | collective-permute-start | bytes 36872 | tf_op jit(solution)/shard_map/ppermute | solution.py:227
  82.2 0.7 copy-start.7

commit v2 on v1

v2 whole, which is shorter than its diff:
```python
import functools

import jax
import jax.numpy as jnp
from jax import lax
from jax.experimental import pallas as pl
from jax.experimental.pallas import tpu as pltpu
from jax.sharding import PartitionSpec as P

CIN = 16
HID = 64
KIN = CIN + HID
GATES = 4 * HID
ROWS = 8
COLS = 128
TW = 4
BAND = 4
WIDE = 3 * KIN
LINE = 256
CHUNK = 16
TAPS = 3 * WIDE
DEEP = 3 * LINE
ROW = TW * COLS

F32 = jnp.float32
BF16 = jnp.bfloat16


def load_rows(stage, tile, row, count, start=0):
    return stage[tile, pl.ds(row + start * ROWS, count, stride=ROWS), :]


def build_row(patch_ref, line, pieces, lane):
    zero = jnp.zeros((KIN, COLS), F32)
    right = [pltpu.roll(piece, 1, 1) for piece in pieces]
    left = [pltpu.roll(piece, COLS - 1, 1) for piece in pieces]
    for tile in range(TW):
        before = right[tile - 1] if tile else zero
        after = left[tile + 1] if tile < TW - 1 else zero
        shifted = (
            jnp.where(lane == 0, before, right[tile]),
            pieces[tile],
            jnp.where(lane == COLS - 1, after, left[tile]),
        )
        span = slice(tile * COLS, (tile + 1) * COLS)
        for offset, value in enumerate(shifted):
            patch_ref[line * LINE + offset * KIN : line * LINE + (offset + 1) * KIN, span] = value.astype(BF16)


def edge_kernel(*refs):
    forcing_refs, hidden_refs = refs[:3], refs[3:6]
    near_ref, far_ref, ending_0, leading_2, ending_2, leading_3 = refs[6:12]
    joined_ref = refs[12]
    odd = lax.rem(lax.axis_index("space"), 2) == 1
    for tile in range(TW):
        for which in range(3):
            slot = which * TW + tile
            joined_ref[slot, : CIN * ROWS, :] = forcing_refs[which][tile].astype(F32).reshape(CIN * ROWS, COLS)
            joined_ref[slot, CIN * ROWS :, :] = hidden_refs[which][tile].astype(F32).reshape(HID * ROWS, COLS)
        first_row = load_rows(joined_ref, tile, 0, KIN)
        last_row = load_rows(joined_ref, 2 * TW + tile, ROWS - 1, KIN)
        near_ref[tile] = jnp.where(odd, first_row, last_row).astype(BF16)
        far_ref[tile] = jnp.where(odd, last_row, first_row).astype(BF16)
        ending_0[tile] = load_rows(joined_ref, tile, ROWS - 1, KIN).astype(BF16)
        leading_2[tile] = load_rows(joined_ref, TW + tile, 0, KIN).astype(BF16)
        ending_2[tile] = load_rows(joined_ref, TW + tile, ROWS - 1, KIN).astype(BF16)
        leading_3[tile] = load_rows(joined_ref, 2 * TW + tile, 0, KIN).astype(BF16)


def edges(forcing, hidden):
    def block(channels, band_row):
        return pl.BlockSpec((TW, channels, ROWS, COLS), lambda part: (band_row, 0, 0, 0))

    shape = jax.ShapeDtypeStruct((TW, KIN, COLS), BF16)
    picked = (0, 2, 3)
    return pl.pallas_call(
        edge_kernel,
        grid=(1,),
        in_specs=[block(CIN, i) for i in picked] + [block(HID, i) for i in picked],
        out_specs=[pl.BlockSpec(memory_space=pltpu.VMEM)] * 6,
        out_shape=[shape] * 6,
        scratch_shapes=[pltpu.VMEM((3 * TW, KIN * ROWS, COLS), F32)],
        compiler_params=pltpu.CompilerParams(vmem_limit_bytes=24 << 20),
        cost_estimate=pl.CostEstimate(flops=0, bytes_accessed=3 << 20, transcendentals=0),
        name="edges",
    )(forcing, forcing, forcing, hidden, hidden, hidden)


def prepare(weight_ref, bias_ref, w_ref, patch_ref, wide_ref):
    wide_ref[...] = jnp.zeros((DEEP, GATES), F32)
    for tap in range(3):
        wide_ref[tap * LINE : tap * LINE + WIDE, :] = weight_ref[tap * WIDE : (tap + 1) * WIDE, :].astype(F32)
    rest = bias_ref[...]
    for piece in range(3):
        value = rest.astype(BF16).astype(F32)
        wide_ref[WIDE + piece : WIDE + piece + 1, :] = value
        rest = rest - value
    gate = lax.broadcasted_iota(jnp.int32, (GATES, 1), 0)
    w_ref[...] = (wide_ref[...].T * jnp.where(gate < 3 * HID, 0.5, 1.0)).astype(BF16)


def fill_ones(patch_ref):
    index = lax.broadcasted_iota(jnp.int32, (LINE - WIDE, ROW), 0)
    ones = jnp.where(index < 3, 1.0, 0.0).astype(BF16)
    for line in range(ROWS + 2):
        patch_ref[line * LINE + WIDE : (line + 1) * LINE, :] = ones


def gates_of_row(pre_ref, before_ref, up_ref, hidden_new, cell_new, grad_ref, row):
    for tile in range(TW):
        span = slice(tile * COLS, (tile + 1) * COLS)
        out_span = slice(row * ROW + tile * COLS, row * ROW + (tile + 1) * COLS)
        for start in range(0, HID, CHUNK):
            in_half, forget_half, out_half, candidate = [
                jnp.tanh(pre_ref[k * HID + start : k * HID + start + CHUNK, span]) for k in range(4)
            ]
            in_gate, forget_gate, out_gate = [0.5 * half + 0.5 for half in (in_half, forget_half, out_half)]
            cell_before = load_rows(before_ref, tile, row, CHUNK, start)
            upstream = load_rows(up_ref, tile, row, CHUNK, start)
            kept = forget_gate * cell_before
            cell_full = kept + in_gate * candidate
            squashed = jnp.tanh(cell_full)
            place = pl.ds(row + start * ROWS, CHUNK, stride=ROWS)
            hidden_new[tile, place, :] = out_gate * squashed
            cell_new[tile, place, :] = cell_full
            raised = upstream * out_gate
            d_cell = raised * (1.0 - squashed * squashed)
            d_in = d_cell * in_gate
            parts = [
                d_in * candidate * (1.0 - in_gate),
                d_cell * kept * (1.0 - forget_gate),
                raised * squashed * (1.0 - out_gate),
                d_in * (1.0 - candidate * candidate),
            ]
            for k, part in enumerate(parts):
                grad_ref[k * HID + start : k * HID + start + CHUNK, out_span] = part.astype(BF16)


def compute_kernel(
    first, step, last,
    worker_ref,
    *rest,
):
    if last:
        (forcing_buf, hidden_buf, cell_buf, grad_buf, near_halo, leading_1, ending_2, far_halo,
         w_ref, acc_in_ref, _, _, hidden_hbm_out, cell_hbm_out, own_out, other_out) = rest[:16]
        scratch = rest[16:]
    else:
        sources = rest[:4]
        (ending_0, leading_2, leading_3, weight_ref, bias_ref,
         hidden_hbm_out, cell_hbm_out, sum_out, w_ref, leading_1) = rest[4:14]
        ahead = rest[14:18]
        buffers, (in_sem, ahead_sem), scratch = rest[18:22], rest[22:24], rest[24:]
        forcing_buf, hidden_buf, cell_buf, grad_buf = buffers
    (hidden_res, cell_res, out_sem,
     patch_ref, joined_ref, before_ref, up_ref, hidden_new, cell_new,
     pre_a, pre_b, grad_ref, total_ref) = scratch
    part = pl.program_id(0)
    home = lax.axis_index("space")
    base = home * (BAND * TW) + (first + part * step) * TW

    def fetch(which, index):
        return pltpu.make_async_copy(
            sources[which].at[pl.ds((first + index * step) * TW, TW)], buffers[which].at[index], in_sem.at[which, index]
        )

    def fetch_ahead(which, index):
        return pltpu.make_async_copy(
            sources[which].at[pl.ds(index * (BAND - 1) * TW, TW)], ahead[which].at[index], ahead_sem.at[which, index]
        )

    def flush(which, index):
        hbm, buf = ((hidden_hbm_out, hidden_res), (cell_hbm_out, cell_res))[which]
        return pltpu.make_async_copy(
            buf.at[index], hbm.at[pl.ds((first + index * step) * TW, TW)], out_sem.at[which, index]
        )

    @pl.when(part == 0)
    def _():
        if not last:
            for which in range(4):
                fetch(which, 0).start()
        fill_ones(patch_ref)
        if last:
            total_ref[...] = acc_in_ref[...]
        else:
            prepare(weight_ref, bias_ref, w_ref, patch_ref, total_ref)
            total_ref[...] = jnp.zeros_like(total_ref)

    if not last:
        @pl.when(part == 1)
        def _():
            patch_ref[:WIDE, :] = patch_ref[ROWS * LINE : ROWS * LINE + WIDE, :]

    if not last:
        fetch(0, part).wait()
        fetch(1, part).wait()
    lane = lax.broadcasted_iota(jnp.int32, (KIN, COLS), 1)
    for tile in range(TW):
        joined_ref[tile, : CIN * ROWS, :] = forcing_buf[part, tile].astype(F32).reshape(CIN * ROWS, COLS)
        joined_ref[tile, CIN * ROWS :, :] = hidden_buf[part, tile].astype(F32).reshape(HID * ROWS, COLS)
    if last:
        odd = lax.rem(home, 2) == 1
        near = [near_halo[t].astype(F32) for t in range(TW)]
        far = [far_halo[t].astype(F32) for t in range(TW)]
        above = [
            jnp.where(part == 0, jnp.where(odd, near[t], far[t]), ending_2[t].astype(F32)) for t in range(TW)
        ]
        below = [
            jnp.where(part == 0, leading_1[t].astype(F32), jnp.where(odd, far[t], near[t])) for t in range(TW)
        ]
        build_row(patch_ref, 0, above, lane)
    else:
        below = [jnp.where(part == 0, leading_2[t].astype(F32), leading_3[t].astype(F32)) for t in range(TW)]

        @pl.when(part == 0)
        def _():
            build_row(patch_ref, 0, [ending_0[t].astype(F32) for t in range(TW)], lane)
            for tile in range(TW):
                leading_1[tile] = load_rows(joined_ref, tile, 0, KIN).astype(BF16)

    if not last:
        fetch(2, part).wait()
        fetch(3, part).wait()

        @pl.when(part == 0)
        def _():
            for which in range(4):
                fetch(which, 1).start()

        @pl.when(part == 1)
        def _():
            for index in range(2):
                for which in range(4):
                    fetch_ahead(which, index).start()


    def build(line):
        if line == ROWS + 1:
            pieces = below
        else:
            pieces = [load_rows(joined_ref, tile, line - 1, KIN) for tile in range(TW)]
        build_row(patch_ref, line, pieces, lane)

    pres = (pre_a, pre_b)

    def forward(row):
        pres[row % 2][...] = jnp.dot(
            w_ref[...], patch_ref[row * LINE : row * LINE + DEEP, :], preferred_element_type=F32
        )

    def backward():
        left = jnp.concatenate([patch_ref[row * LINE : row * LINE + DEEP, :] for row in range(ROWS)], axis=1)
        total_ref[...] += lax.dot_general(
            left, grad_ref[...], (((1,), (1,)), ((), ())), preferred_element_type=F32
        )

    for line in range(1, 3):
        build(line)
    forward(0)
    for tile in range(TW):
        before_ref[tile] = cell_buf[part, tile].astype(F32).reshape(HID * ROWS, COLS)
        live = worker_ref[base + tile] >= 0
        up = grad_buf[part, tile].astype(F32).reshape(HID * ROWS, COLS)
        up_ref[tile] = jnp.where(live, up, 0.0)
    for row in range(ROWS):
        if row + 1 < ROWS:
            build(row + 3)
            forward(row + 1)
        gates_of_row(pres[row % 2], before_ref, up_ref, hidden_new, cell_new, grad_ref, row)

    for tile in range(TW):
        live = worker_ref[base + tile] >= 0
        fresh = hidden_new[tile].reshape(HID, ROWS, COLS).astype(BF16)
        hidden_res[part, tile] = jnp.where(live, fresh, hidden_buf[part, tile])
        fresh = cell_new[tile].reshape(HID, ROWS, COLS).astype(BF16)
        cell_res[part, tile] = jnp.where(live, fresh, cell_buf[part, tile])
    flush(0, part).start()
    flush(1, part).start()
    backward()

    @pl.when(part == 1)
    def _():
        if last:
            packed = jnp.concatenate(
                [total_ref[tap * LINE : tap * LINE + WIDE, :] for tap in range(3)]
                + [total_ref[WIDE:LINE, :], jnp.zeros((DEEP - TAPS - LINE + WIDE, GATES), F32)],
                axis=0,
            )
            turned = packed.T
            odd = lax.rem(home, 2) == 1
            for pair in range(GATES // (2 * ROWS)):
                even_half = turned[2 * pair * ROWS : (2 * pair + 1) * ROWS]
                odd_half = turned[(2 * pair + 1) * ROWS : (2 * pair + 2) * ROWS]
                own_out[pair] = jnp.where(odd, odd_half, even_half)
                other_out[pair] = jnp.where(odd, even_half, odd_half).astype(BF16)
        else:
            sum_out[...] = total_ref[...]
            for index in range(2):
                for which in range(4):
                    fetch_ahead(which, index).wait()
        for index in range(2):
            for which in range(2):
                flush(which, index).wait()


def compute(first, step, worker, carried, hidden, last):
    resident = pl.BlockSpec(memory_space=pltpu.VMEM)
    anywhere = pl.BlockSpec(memory_space=pl.ANY)
    operands = [worker] + carried
    state = jax.ShapeDtypeStruct(hidden.shape, BF16)
    small = (2, TW, CIN, ROWS, COLS)
    large = (2, TW, HID, ROWS, COLS)
    out_shape = [state, state]
    aliases = {}
    scratch = []
    if last:
        in_specs = [resident] * 10 + [anywhere] * 2
        aliases = {11: 0, 12: 1}
        out_shape.append(jax.ShapeDtypeStruct((GATES // (2 * ROWS), ROWS, DEEP), F32))
        out_shape.append(jax.ShapeDtypeStruct((GATES // (2 * ROWS), ROWS, DEEP), BF16))
    else:
        in_specs = [anywhere] * 4 + [resident] * 5
        out_shape.append(jax.ShapeDtypeStruct((DEEP, GATES), F32))
        out_shape.append(jax.ShapeDtypeStruct((GATES, DEEP), BF16))
        out_shape.append(jax.ShapeDtypeStruct((TW, KIN, COLS), BF16))
        out_shape += [jax.ShapeDtypeStruct(shape, BF16) for shape in (small, large, large, large)]
        scratch = [pltpu.VMEM(shape, BF16) for shape in (small, large, large, large)]
        scratch += [pltpu.SemaphoreType.DMA((4, 2)), pltpu.SemaphoreType.DMA((4, 2))]
    stage = pltpu.VMEM((TW, HID * ROWS, COLS), F32)
    return pl.pallas_call(
        functools.partial(compute_kernel, first, step, last),
        grid_spec=pltpu.PrefetchScalarGridSpec(
            num_scalar_prefetch=1,
            grid=(2,),
            in_specs=in_specs,
            out_specs=[anywhere, anywhere] + [resident] * (len(out_shape) - 2),
            scratch_shapes=scratch + [
                pltpu.VMEM(large, BF16),
                pltpu.VMEM(large, BF16),
                pltpu.SemaphoreType.DMA((2, 2)),
                pltpu.VMEM(((ROWS + 2) * LINE, ROW), BF16),
                pltpu.VMEM((TW, KIN * ROWS, COLS), F32),
                stage, stage, stage, stage,
                pltpu.VMEM((GATES, ROW), F32),
                pltpu.VMEM((GATES, ROW), F32),
                pltpu.VMEM((GATES, ROWS * ROW), BF16),
                pltpu.VMEM((DEEP, GATES), F32),
            ],
        ),
        out_shape=out_shape,
        input_output_aliases=aliases,
        compiler_params=pltpu.CompilerParams(vmem_limit_bytes=40 << 20),
        cost_estimate=pl.CostEstimate(
            flops=8 * TW * ROWS * COLS * TAPS * GATES, bytes_accessed=6 << 20, transcendentals=0
        ),
        name="second" if last else "first",
    )(*operands)


def shards(forcing, hidden_prev, cell_prev, hidden_grad, w_gates, gate_bias, worker):
    size = lax.axis_size("space")
    forcing, hidden, cell, grad = [
        pltpu.with_memory_space_constraint(array[0], pltpu.HBM)
        for array in (forcing, hidden_prev, cell_prev, hidden_grad)
    ]
    near, far, ending_0, leading_2, ending_2, leading_3 = edges(forcing, hidden)
    near_halo = lax.ppermute(near, "space", [(i, i ^ 1) for i in range(size)])
    far_pairs = [(i, i + 1) for i in range(1, size - 1, 2)]
    far_halo = lax.ppermute(far, "space", far_pairs + [(j, i) for i, j in far_pairs])
    tiles = worker[0]
    hidden_part, cell_part, total, w, leading_1, *ahead = compute(
        1, 1, tiles,
        [forcing, hidden, cell, grad, ending_0, leading_2, leading_3, w_gates.T, gate_bias[None, :]], hidden, False,
    )
    hidden_next, cell_next, own, other = compute(
        0, 3, tiles,
        [*ahead, near_halo, leading_1, ending_2, far_halo, w, total, hidden_part, cell_part], hidden, True,
    )
    half = own + lax.ppermute(other, "space", [(i, i ^ 1) for i in range(size)]).astype(F32)
    groups = [list(range(core, size, 2)) for core in range(2)]
    pieces = lax.all_to_all(half.astype(BF16), "space", 0, 0, tiled=True, axis_index_groups=groups)
    mine = jnp.sum(pieces.astype(F32), axis=0).astype(BF16)
    years = lax.axis_size("dp")
    total = mine.astype(F32)
    for k in range(1, years):
        other = lax.ppermute(mine, "dp", [(i, (i + k) % years) for i in range(years)])
        total = total + other.astype(F32)
    return hidden_next[None], cell_next[None], total[:, :TAPS], total[:, TAPS]


def solution(mesh):
    tiles = P("dp", "space", None, None, None)
    return jax.shard_map(
        shards,
        mesh=mesh,
        in_specs=(tiles, tiles, tiles, tiles, P(), P(), P("dp", None)),
        out_specs=(tiles, tiles, P("space", None), P("space")),
        check_vma=False,
    )
```

time: 83.4 us -> 58.1 us (0.70)
  Pallas kernels: 36.1 us -> 26.7 us
  local copies, waits for them, and re-layouts: 7.35 us -> 0.71 us
  blocking collectives: 20.9 us -> 15.8 us
  other arithmetic: 3.32 us -> 0.08 us
  waiting for transfers between devices: 6.67 us -> 5.1 us
  starting transfers between devices: 7.82 us -> 8.74 us
    pallas_call x2, Pallas kernels: 36.1 us -> 24.8 us  [compute(): pl.pallas_call(functools.partial(compute_kernel, first, step, last), grid...]
    unnamed x20 -> x8, local copies, waits for them, and re-layouts: 6.47 us -> 0.02 us
    all_to_all x1, blocking collectives: 20.9 us -> 15.8 us  [shards(): lax.all_to_all(half.astype(BF16), 'space', 0, 0, tiled=True, axis_index_g...]
    concatenate x2 -> x0, other arithmetic: 1.96 us -> none  [the longest x1 1.04 us: shards(): jnp.concatenate([joined_f[:, :, :, ROWS - 1], joined_h[:, :, :, ROWS - 1]...]
    pallas_call x0 -> x1, Pallas kernels: none -> 1.93 us  [edges(): pl.pallas_call(edge_kernel, grid=(1,), in_specs=[block(CIN, i) for i in p...]
    ppermute x2 -> x3, waiting for transfers between devices: 2.65 us -> 1.08 us  [the longest x1 1.07 us: shards(): lax.ppermute(other, 'space', [(i, i ^ 1) for i in range(size)]).astype(F32)]
    slice x2 -> x0, other arithmetic: 1.28 us -> none  [the longest x1 0.64 us: shards(): before = lax.ppermute(ending[BAND - 1:], 'space', up)]
    ppermute x2 -> x3, starting transfers between devices: 3.31 us -> 4.22 us  [the longest x1 3.47 us: shards(): lax.ppermute(other, 'space', [(i, i ^ 1) for i in range(size)]).astype(F32)]
  transfers between devices with their start and end apart: 5 -> 6, of which waited for: 3 -> 3; matrix products, arithmetic and copies ran while one was open for 2% -> 0% of each run, Pallas kernels for 0% -> 23%
where the time goes in v2:
time: 58.1 us; the launch traced here: 57.9 us
  Pallas kernels  26.7 us (46%)
  blocking collectives  15.8 us (27%)
  starting transfers between devices  8.74 us (15%)
  waiting for transfers between devices  5.1 us (9%)
  between operations  0.75 us (1%)
  local copies, waits for them, and re-layouts  0.71 us (1%)
    pallas_call x2, Pallas kernels, compute(): pl.pallas_call(functools.partial(compute_kernel, first, step, last), grid...  24.8 us
    all_to_all x1, blocking collectives, shards(): lax.all_to_all(half.astype(BF16), 'space', 0, 0, tiled=True, axis_index_g...  15.8 us
    ppermute x3, starting transfers between devices, shards(): lax.ppermute(mine, 'dp', [(i, (i + k) % years) for i in range(years)])  4.52 us
    ppermute x3, waiting for transfers between devices, shards(): lax.ppermute(mine, 'dp', [(i, (i + k) % years) for i in range(years)])  4.02 us
    ppermute x1, starting transfers between devices, shards(): lax.ppermute(other, 'space', [(i, i ^ 1) for i in range(size)]).astype(F32)  3.47 us
    pallas_call x1, Pallas kernels, edges(): pl.pallas_call(edge_kernel, grid=(1,), in_specs=[block(CIN, i) for i in p...  1.93 us
  transfers between devices with their start and end apart: 6, of which 3 were waited for; matrix products, arithmetic and copies ran while one was open for 0% of the time, Pallas kernels for 23%

profile of v2, /device:TPU:0, one launch (start us, length us, event | category | flops | bytes accessed | tf_op | source)
XLA Modules:
  0.0 57.9 jit_solution(13099731284325481812)
XLA Ops:
  0.6 0.0 copy-start
  0.6 0.0 copy-start.1
  0.7 0.0 copy-start.2
  0.7 1.9 %edges.1 = (bf16[4,80,128]{2,1,0:T(8,128)(2,1)S(1)}, bf16[4,80,128]{2,1,0:T(8,128)(2,1)S(1)}, bf16[4,80,128]{2,1,0:T(8,128)(2,1)S(1)}, bf16[4,80,128]{2,1,0:T(8,...) custom-call(bf16[16,16,8,128]{3,2,1,0:T(8,128)(2,1)} %bitcast.18, ...), custom_call_target="tpu_custom_call" | custom-call | bytes 3145728 | tf_op jit(solution)/shard_map/edges/pallas_call | solution.py:76
  2.6 0.1 collective-permute-start
  2.7 0.7 %collective-permute-start.1 = (bf16[4,80,128]{2,1,0:T(8,128)(2,1)S(1)}, bf16[4,80,128]{2,1,0:T(8,128)(2,1)S(1)}, u32[]{:S(2)}, u32[]{:S(2)}) collective-permute-start(bf16[4,80,128]{2,1,0:T(8,128)(2,1)S(1)} %get-tuple-element.33), channel_id=1, source_target_pairs={{4,8},{12,16},{20,24},{28,32},{36,40},{44,48},{52,56},{60,64},{68,... | collective-permute-start | bytes 245768 | tf_op jit(solution)/shard_map/ppermute | solution.py:370
  3.4 0.0 copy-done
  3.4 0.0 copy-done.1
  3.4 0.0 copy-done.2
  3.4 13.3 %first.1 = (bf16[16,64,8,128]{3,2,1,0:T(8,128)(2,1)}, bf16[16,64,8,128]{3,2,1,0:T(8,128)(2,1)}, f32[768,256]{1,0:T(8,128)S(1)}, bf16[256,768]{1,0:T(8,128)(2,1)S...) custom-call(s32[512]{0:T(512)S(1)} %bitcast.11, ...), custom_call_target="tpu_custom_call" | custom-call | flops 6039797760 | bytes 6291456 | tf_op jit(solution)/shard_map/first/pallas_call | solution.py:331
  16.7 0.0 collective-permute-done.rest_4_
  16.7 0.0 collective-permute-done.1.rest_7_
  16.7 11.5 %second.1 = (bf16[16,64,8,128]{3,2,1,0:T(8,128)(2,1)}, bf16[16,64,8,128]{3,2,1,0:T(8,128)(2,1)}, f32[16,8,768]{2,1,0:T(8,128)S(1)}, bf16[16,8,768]{2,1,0:T(8,128)(2,1)S(1)}) custom-call(s32[512]{0:T(512)S(1)} %bitcast.12, bf16[2,4,16,8,128]{4,3,2,1,0:T(8,128)(2,1)S(1)} %get-tuple-element.26.rest_0_, ...), custom_call_target="tpu_custom_call", output_to_operand_aliasing={{0}: (11, {}), {1}: (12, {})} | custom-call | flops 6039797760 | bytes 6291456 | tf_op jit(solution)/shard_map/second/pallas_call | solution.py:331
  28.2 3.5 %collective-permute-start.2 = (bf16[16,8,768]{2,1,0:T(8,128)(2,1)S(1)}, bf16[16,8,768]{2,1,0:T(8,128)(2,1)S(1)}, u32[]{:S(2)}, u32[]{:S(2)}) collective-permute-start(bf16[16,8,768]{2,1,0:T(8,128)(2,1)S(1)} %get-tuple-element.41), channel_id=1, source_target_pairs={{0,4},{4,0},{8,12},{12,8},{16,20},{20,16},{24,28},{28,24},{32,36},... | collective-permute-start | bytes 589832 | tf_op jit(solution)/shard_map/ppermute | solution.py:380
  31.7 1.1 %collective-permute-done.2 = bf16[16,8,768]{2,1,0:T(8,128)(2,1)S(1)} collective-permute-done((bf16[16,8,768]{2,1,0:T(8,128)(2,1)S(1)}, bf16[16,8,768]{2,1,0:T(8,128)(2,1)S(1)}, u32[]{:S(2)}, u32[]{:S(2)}) %collective-permute-start.2) | collective-permute-done | bytes 196640 | tf_op jit(solution)/shard_map/ppermute | solution.py:380
  32.8 15.8 %all_to_all.5 = bf16[16,8,768]{2,1,0:T(8,128)(2,1)S(1)} all-to-all(bf16[16,8,768]{2,1,0:T(8,128)(2,1)S(1)} %add_convert_fusion), channel_id=1, replica_groups={{0,8,16,24,32,40,48,56,64,72,80,88,96,104,112,120},{4,12,20,28,36,44,52..., dimensions={0} | all-to-all | bytes 393216 | tf_op jit(solution)/shard_map/all_to_all | solution.py:382
  48.6 2.8 %collective-permute-start.5 = (bf16[8,768]{1,0:T(8,128)(2,1)S(1)}, bf16[8,768]{1,0:T(8,128)(2,1)S(1)}, u32[]{:S(2)}, u32[]{:S(2)}) collective-permute-start(bf16[8,768]{1,0:T(8,128)(2,1)S(1)} %reduce_sum.12), channel_id=1, source_target_pairs={{0,3},{1,0},{2,1},{3,2},{4,7},{5,4},{6,5},{7,6},{8,11},{9,8},{10,9... | collective-permute-start | bytes 36872 | tf_op jit(solution)/shard_map/ppermute | solution.py:387
  51.4 0.8 %collective-permute-start.4 = (bf16[8,768]{1,0:T(8,128)(2,1)S(1)}, bf16[8,768]{1,0:T(8,128)(2,1)S(1)}, u32[]{:S(2)}, u32[]{:S(2)}) collective-permute-start(bf16[8,768]{1,0:T(8,128)(2,1)S(1)} %reduce_sum.12), channel_id=1, source_target_pairs={{0,2},{1,3},{2,0},{3,1},{4,6},{5,7},{6,4},{7,5},{8,10},{9,11},{10,... | collective-permute-start | bytes 36872 | tf_op jit(solution)/shard_map/ppermute | solution.py:387
  52.3 0.9 %collective-permute-start.3 = (bf16[8,768]{1,0:T(8,128)(2,1)S(1)}, bf16[8,768]{1,0:T(8,128)(2,1)S(1)}, u32[]{:S(2)}, u32[]{:S(2)}) collective-permute-start(bf16[8,768]{1,0:T(8,128)(2,1)S(1)} %reduce_sum.12), channel_id=1, source_target_pairs={{0,1},{1,2},{2,3},{3,0},{4,5},{5,6},{6,7},{7,4},{8,9},{9,10},{10,1... | collective-permute-start | bytes 36872 | tf_op jit(solution)/shard_map/ppermute | solution.py:387
  53.1 0.0 collective-permute-done.5
  53.1 3.5 %collective-permute-done.4 = bf16[8,768]{1,0:T(8,128)(2,1)S(1)} collective-permute-done((bf16[8,768]{1,0:T(8,128)(2,1)S(1)}, bf16[8,768]{1,0:T(8,128)(2,1)S(1)}, u32[]{:S(2)}, u32[]{:S(2)}) %collective-permute-start.4) | collective-permute-done | bytes 12320 | tf_op jit(solution)/shard_map/ppermute | solution.py:387
  56.6 0.5 collective-permute-done.3
  57.2 0.0 copy-start.3
  57.2 0.7 %slice_reduce_fusion = f32[8]{0:T(128)} fusion(f32[8,768]{1,0:T(8,128)S(1)} %convert_add_fusion), kind=kLoop, calls=%fused_computation.2 | loop fusion | bytes 64 | tf_op jit(solution)/shard_map/slice | solution.py:389
  (4 shorter events, 0.1 us)
Async XLA Ops:
  0.6 2.7 %copy-start = (bf16[256,720]{0,1:T(8,128)(2,1)S(1)}, bf16[256,720]{0,1:T(8,128)(2,1)}, u32[]{:S(2)}) copy-start(bf16[256,720]{0,1:T(8,128)(2,1)} %param.11) | copy-start | bytes 1105924
  0.6 2.7 %copy-start.1 = (s32[1,512]{1,0:T(1,128)S(1)}, s32[1,512]{1,0:T(1,128)}, u32[]{:S(2)}) copy-start(s32[1,512]{1,0:T(1,128)} %param.13) | copy-start | bytes 6148
  0.7 2.7 %copy-start.2 = (f32[256]{0:T(256)S(1)}, f32[256]{0:T(256)}, u32[]{:S(2)}) copy-start(f32[256]{0:T(256)} %param.12) | copy-start | bytes 3076
  2.6 14.1 %collective-permute-start = (bf16[4,80,128]{2,1,0:T(8,128)(2,1)S(1)}, bf16[4,80,128]{2,1,0:T(8,128)(2,1)S(1)}, u32[]{:S(2)}, u32[]{:S(2)}) collective-permute-start(bf16[4,80,128]{2,1,0:T(8,128)(2,1)S(1)} %get-tuple-element.30), channel_id=1, source_target_pairs={{0,4},{4,0},{8,12},{12,8},{16,20},{20,16},{24,28},{28,24},{32,36},... | collective-permute-start | bytes 245768 | tf_op jit(solution)/shard_map/ppermute | solution.py:368
  2.7 14.0 %collective-permute-start.1 = (bf16[4,80,128]{2,1,0:T(8,128)(2,1)S(1)}, bf16[4,80,128]{2,1,0:T(8,128)(2,1)S(1)}, u32[]{:S(2)}, u32[]{:S(2)}) collective-permute-start(bf16[4,80,128]{2,1,0:T(8,128)(2,1)S(1)} %get-tuple-element.33), channel_id=1, source_target_pairs={{4,8},{12,16},{20,24},{28,32},{36,40},{44,48},{52,56},{60,64},{68,... | collective-permute-start | bytes 245768 | tf_op jit(solution)/shard_map/ppermute | solution.py:370
  28.2 4.5 %collective-permute-start.2 = (bf16[16,8,768]{2,1,0:T(8,128)(2,1)S(1)}, bf16[16,8,768]{2,1,0:T(8,128)(2,1)S(1)}, u32[]{:S(2)}, u32[]{:S(2)}) collective-permute-start(bf16[16,8,768]{2,1,0:T(8,128)(2,1)S(1)} %get-tuple-element.41), channel_id=1, source_target_pairs={{0,4},{4,0},{8,12},{12,8},{16,20},{20,16},{24,28},{28,24},{32,36},... | collective-permute-start | bytes 589832 | tf_op jit(solution)/shard_map/ppermute | solution.py:380
  48.6 4.5 %collective-permute-start.5 = (bf16[8,768]{1,0:T(8,128)(2,1)S(1)}, bf16[8,768]{1,0:T(8,128)(2,1)S(1)}, u32[]{:S(2)}, u32[]{:S(2)}) collective-permute-start(bf16[8,768]{1,0:T(8,128)(2,1)S(1)} %reduce_sum.12), channel_id=1, source_target_pairs={{0,3},{1,0},{2,1},{3,2},{4,7},{5,4},{6,5},{7,6},{8,11},{9,8},{10,9... | collective-permute-start | bytes 36872 | tf_op jit(solution)/shard_map/ppermute | solution.py:387
  51.4 5.2 %collective-permute-start.4 = (bf16[8,768]{1,0:T(8,128)(2,1)S(1)}, bf16[8,768]{1,0:T(8,128)(2,1)S(1)}, u32[]{:S(2)}, u32[]{:S(2)}) collective-permute-start(bf16[8,768]{1,0:T(8,128)(2,1)S(1)} %reduce_sum.12), channel_id=1, source_target_pairs={{0,2},{1,3},{2,0},{3,1},{4,6},{5,7},{6,4},{7,5},{8,10},{9,11},{10,... | collective-permute-start | bytes 36872 | tf_op jit(solution)/shard_map/ppermute | solution.py:387
  52.3 4.9 %collective-permute-start.3 = (bf16[8,768]{1,0:T(8,128)(2,1)S(1)}, bf16[8,768]{1,0:T(8,128)(2,1)S(1)}, u32[]{:S(2)}, u32[]{:S(2)}) collective-permute-start(bf16[8,768]{1,0:T(8,128)(2,1)S(1)} %reduce_sum.12), channel_id=1, source_target_pairs={{0,1},{1,2},{2,3},{3,0},{4,5},{5,6},{6,7},{7,4},{8,9},{9,10},{10,1... | collective-permute-start | bytes 36872 | tf_op jit(solution)/shard_map/ppermute | solution.py:387
  57.2 0.7 %copy-start.3 = (f32[8,768]{1,0:T(8,128)}, f32[8,768]{1,0:T(8,128)S(1)}, u32[]{:S(2)}) copy-start(f32[8,768]{1,0:T(8,128)S(1)} %convert_add_fusion) | copy-start | bytes 73732

commit v3 on v2

v3 whole, which is shorter than its diff:
```python
import functools

import jax
import jax.numpy as jnp
from jax import lax
from jax.experimental import pallas as pl
from jax.experimental.pallas import tpu as pltpu
from jax.sharding import PartitionSpec as P

CIN = 16
HID = 64
KIN = CIN + HID
GATES = 4 * HID
ROWS = 8
COLS = 128
TW = 4
BAND = 4
WIDE = 3 * KIN
LINE = 256
CHUNK = 16
TAPS = 3 * WIDE
DEEP = 3 * LINE
ROW = TW * COLS

F32 = jnp.float32
BF16 = jnp.bfloat16


def load_rows(stage, tile, row, count, start=0):
    return stage[tile, pl.ds(row + start * ROWS, count, stride=ROWS), :]


def build_row(patch_ref, line, pieces, lane):
    zero = jnp.zeros((KIN, COLS), F32)
    right = [pltpu.roll(piece, 1, 1) for piece in pieces]
    left = [pltpu.roll(piece, COLS - 1, 1) for piece in pieces]
    for tile in range(TW):
        before = right[tile - 1] if tile else zero
        after = left[tile + 1] if tile < TW - 1 else zero
        shifted = (
            jnp.where(lane == 0, before, right[tile]),
            pieces[tile],
            jnp.where(lane == COLS - 1, after, left[tile]),
        )
        span = slice(tile * COLS, (tile + 1) * COLS)
        for offset, value in enumerate(shifted):
            patch_ref[line * LINE + offset * KIN : line * LINE + (offset + 1) * KIN, span] = value.astype(BF16)


def edge_kernel(forcing_hbm, hidden_hbm, near_ref, far_ref, ending_0, leading_3, forcing_buf, hidden_buf, joined_ref, sem):
    odd = lax.rem(lax.axis_index("space"), 2) == 1
    copies = []
    for slot, band_row in ((0, 0), (2, BAND - 1), (1, 1)):
        for which, (hbm, buf) in enumerate(((forcing_hbm, forcing_buf), (hidden_hbm, hidden_buf))):
            copies.append(
                pltpu.make_async_copy(hbm.at[pl.ds(band_row * TW, TW)], buf.at[slot], sem.at[which, slot])
            )
            copies[-1].start()
    for copy in copies[:4]:
        copy.wait()
    for tile in range(TW):
        for which in range(2):
            slot = which * TW + tile
            joined_ref[slot, : CIN * ROWS, :] = forcing_buf[2 * which, tile].astype(F32).reshape(CIN * ROWS, COLS)
            joined_ref[slot, CIN * ROWS :, :] = hidden_buf[2 * which, tile].astype(F32).reshape(HID * ROWS, COLS)
        first_row = load_rows(joined_ref, tile, 0, KIN)
        last_row = load_rows(joined_ref, TW + tile, ROWS - 1, KIN)
        near_ref[tile] = jnp.where(odd, first_row, last_row).astype(BF16)
        far_ref[tile] = jnp.where(odd, last_row, first_row).astype(BF16)
        ending_0[tile] = load_rows(joined_ref, tile, ROWS - 1, KIN).astype(BF16)
        leading_3[tile] = load_rows(joined_ref, TW + tile, 0, KIN).astype(BF16)
    for copy in copies[4:]:
        copy.wait()


def edges(forcing, hidden):
    shape = jax.ShapeDtypeStruct((TW, KIN, COLS), BF16)
    return pl.pallas_call(
        edge_kernel,
        in_specs=[pl.BlockSpec(memory_space=pl.ANY)] * 2,
        out_specs=[pl.BlockSpec(memory_space=pltpu.VMEM)] * 6,
        out_shape=[shape] * 4 + [jax.ShapeDtypeStruct((3, TW, n, ROWS, COLS), BF16) for n in (CIN, HID)],
        scratch_shapes=[pltpu.VMEM((2 * TW, KIN * ROWS, COLS), F32), pltpu.SemaphoreType.DMA((2, 3))],
        compiler_params=pltpu.CompilerParams(vmem_limit_bytes=24 << 20),
        cost_estimate=pl.CostEstimate(flops=0, bytes_accessed=3 << 20, transcendentals=0),
        name="edges",
    )(forcing, hidden)


def prepare(weight_ref, bias_ref, w_ref, wide_ref):
    wide_ref[...] = jnp.zeros((DEEP, GATES), F32)
    for tap in range(3):
        wide_ref[tap * LINE : tap * LINE + WIDE, :] = weight_ref[tap * WIDE : (tap + 1) * WIDE, :].astype(F32)
    rest = bias_ref[...]
    for piece in range(3):
        value = rest.astype(BF16).astype(F32)
        wide_ref[WIDE + piece : WIDE + piece + 1, :] = value
        rest = rest - value
    gate = lax.broadcasted_iota(jnp.int32, (GATES, 1), 0)
    w_ref[...] = (wide_ref[...].T * jnp.where(gate < 3 * HID, 0.5, 1.0)).astype(BF16)


def fill_ones(patch_ref):
    index = lax.broadcasted_iota(jnp.int32, (LINE - WIDE, ROW), 0)
    ones = jnp.where(index < 3, 1.0, 0.0).astype(BF16)
    for line in range(ROWS + 2):
        patch_ref[line * LINE + WIDE : (line + 1) * LINE, :] = ones


def gates_of_row(pre_ref, before_ref, up_ref, hidden_new, cell_new, grad_ref, row):
    for tile in range(TW):
        span = slice(tile * COLS, (tile + 1) * COLS)
        out_span = slice(row * ROW + tile * COLS, row * ROW + (tile + 1) * COLS)
        for start in range(0, HID, CHUNK):
            in_half, forget_half, out_half, candidate = [
                jnp.tanh(pre_ref[k * HID + start : k * HID + start + CHUNK, span]) for k in range(4)
            ]
            in_gate, forget_gate, out_gate = [0.5 * half + 0.5 for half in (in_half, forget_half, out_half)]
            cell_before = load_rows(before_ref, tile, row, CHUNK, start)
            upstream = load_rows(up_ref, tile, row, CHUNK, start)
            kept = forget_gate * cell_before
            cell_full = kept + in_gate * candidate
            squashed = jnp.tanh(cell_full)
            place = pl.ds(row + start * ROWS, CHUNK, stride=ROWS)
            hidden_new[tile, place, :] = out_gate * squashed
            cell_new[tile, place, :] = cell_full
            raised = upstream * out_gate
            d_cell = raised * (1.0 - squashed * squashed)
            d_in = d_cell * in_gate
            parts = [
                d_in * candidate * (1.0 - in_gate),
                d_cell * kept * (1.0 - forget_gate),
                raised * squashed * (1.0 - out_gate),
                d_in * (1.0 - candidate * candidate),
            ]
            for k, part in enumerate(parts):
                grad_ref[k * HID + start : k * HID + start + CHUNK, out_span] = part.astype(BF16)


def compute_kernel(
    first, step, last,
    worker_ref,
    *rest,
):
    if last:
        (forcing_in, hidden_in, cell_buf, grad_buf, near_halo, leading_1, ending_2, far_halo,
         w_ref, acc_in_ref, _, _, hidden_hbm_out, cell_hbm_out, own_out, other_out) = rest[:16]
        scratch = rest[16:]
        state_of = [(forcing_in.at[2 * part], hidden_in.at[2 * part]) for part in range(2)]
    else:
        sources = rest[:4]
        (forcing_in, hidden_in, ending_0, leading_3, weight_ref, bias_ref,
         hidden_hbm_out, cell_hbm_out, sum_out, w_ref, leading_1, ending_2) = rest[4:16]
        ahead = rest[16:18]
        (forcing_own, hidden_own, cell_buf, grad_buf, in_sem, ahead_sem) = rest[18:24]
        scratch = rest[24:]
        state_of = [(forcing_in.at[1], hidden_in.at[1]), (forcing_own, hidden_own)]
    hidden_res, cell_res, out_sem, total_ref, pre_a, pre_b = scratch[:6]
    stages = scratch[6:]
    home = lax.axis_index("space")
    odd = lax.rem(home, 2) == 1
    pres = (pre_a, pre_b)

    def fetch(which, index):
        buffer = (forcing_own, hidden_own, cell_buf.at[index], grad_buf.at[index])[which]
        return pltpu.make_async_copy(
            sources[which].at[pl.ds((first + index * step) * TW, TW)], buffer, in_sem.at[which, index]
        )

    def fetch_ahead(which, index):
        return pltpu.make_async_copy(
            sources[which + 2].at[pl.ds(index * (BAND - 1) * TW, TW)], ahead[which].at[index], ahead_sem.at[which, index]
        )

    def flush(which, index):
        hbm, buf = ((hidden_hbm_out, hidden_res), (cell_hbm_out, cell_res))[which]
        return pltpu.make_async_copy(
            buf.at[index], hbm.at[pl.ds((first + index * step) * TW, TW)], out_sem.at[which, index]
        )

    def run(patches, grads):
        if not last:
            for which, index in ((2, 0), (3, 0), (0, 1), (1, 1)):
                fetch(which, index).start()
        for patch_ref in patches:
            fill_ones(patch_ref)
        if not last:
            prepare(weight_ref, bias_ref, w_ref, total_ref)
        for part in range(2):
            one_part(part, patches, grads[part], stages[0], *stages[6 * part : 6 * part + 6])
        if last:
            packed = jnp.concatenate(
                [total_ref[tap * LINE : tap * LINE + WIDE, :] for tap in range(3)]
                + [total_ref[WIDE:LINE, :], jnp.zeros((DEEP - TAPS - LINE + WIDE, GATES), F32)],
                axis=0,
            )
            turned = packed.T
            for pair in range(GATES // (2 * ROWS)):
                even_half = turned[2 * pair * ROWS : (2 * pair + 1) * ROWS]
                odd_half = turned[(2 * pair + 1) * ROWS : (2 * pair + 2) * ROWS]
                own_out[pair] = jnp.where(odd, odd_half, even_half)
                other_out[pair] = jnp.where(odd, even_half, odd_half).astype(BF16)
        else:
            sum_out[...] = total_ref[...]
            for index in range(2):
                for which in range(2):
                    fetch_ahead(which, index).wait()
        for index in range(2):
            for which in range(2):
                flush(which, index).wait()

    def one_part(part, patches, grad_ref, joined_0, joined_ref, before_ref, up_ref, hidden_new, cell_new, _):
        patch_ref = patches[part]
        base = home * (BAND * TW) + (first + part * step) * TW
        forcing_buf, hidden_buf = state_of[part]
        lane = lax.broadcasted_iota(jnp.int32, (KIN, COLS), 1)

        def stage(which, into):
            forcing_ref, hidden_ref = state_of[which]
            for tile in range(TW):
                into[tile, : CIN * ROWS, :] = forcing_ref[tile].astype(F32).reshape(CIN * ROWS, COLS)
                into[tile, CIN * ROWS :, :] = hidden_ref[tile].astype(F32).reshape(HID * ROWS, COLS)

        if last or part == 0:
            stage(part, joined_ref)

        def halo(even_ref, odd_ref):
            return [jnp.where(odd, odd_ref[t].astype(F32), even_ref[t].astype(F32)) for t in range(TW)]

        def plain(ref):
            return [ref[t].astype(F32) for t in range(TW)]

        if last:
            above = plain(ending_2) if part else halo(far_halo, near_halo)
            below = halo(near_halo, far_halo) if part else plain(leading_1)
        else:
            above = None if part else plain(ending_0)
            below = plain(leading_3) if part else None
        if above is None:
            patch_ref[:WIDE, :] = patches[0][ROWS * LINE : ROWS * LINE + WIDE, :]
        else:
            build_row(patch_ref, 0, above, lane)

        def build(line):
            if line == ROWS + 1 and below is None:
                pieces = [load_rows(stages[6], tile, 0, KIN) for tile in range(TW)]
            elif line == ROWS + 1:
                pieces = below
            else:
                pieces = [load_rows(joined_ref, tile, line - 1, KIN) for tile in range(TW)]
            build_row(patch_ref, line, pieces, lane)

        def forward(row):
            pres[row % 2][...] = jnp.dot(
                w_ref[...], patch_ref[row * LINE : row * LINE + DEEP, :], preferred_element_type=F32
            )

        for line in range(1, 3):
            build(line)
        forward(0)
        if not last:
            fetch(2, part).wait()
            fetch(3, part).wait()
        for tile in range(TW):
            before_ref[tile] = cell_buf[part, tile].astype(F32).reshape(HID * ROWS, COLS)
            live = worker_ref[base + tile] >= 0
            up = grad_buf[part, tile].astype(F32).reshape(HID * ROWS, COLS)
            up_ref[tile] = jnp.where(live, up, 0.0)
        for row in range(ROWS):
            if not last and row == 1 and part == 0:
                fetch(2, 1).start()
                fetch(3, 1).start()
                fetch(0, 1).wait()
                fetch(1, 1).wait()
            if not last and row == 4 and part == 0:
                stage(1, stages[6])
                for tile in range(TW):
                    leading_1[tile] = load_rows(stages[0], tile, 0, KIN).astype(BF16)
                    ending_2[tile] = load_rows(stages[6], tile, ROWS - 1, KIN).astype(BF16)
            if not last and row == 1 and part == 1:
                for index in range(2):
                    for which in range(2):
                        fetch_ahead(which, index).start()
            if row + 1 < ROWS:
                build(row + 3)
                forward(row + 1)
            gates_of_row(pres[row % 2], before_ref, up_ref, hidden_new, cell_new, grad_ref, row)

        for tile in range(TW):
            live = worker_ref[base + tile] >= 0
            fresh = hidden_new[tile].reshape(HID, ROWS, COLS).astype(BF16)
            hidden_res[part, tile] = jnp.where(live, fresh, hidden_buf[tile])
            fresh = cell_new[tile].reshape(HID, ROWS, COLS).astype(BF16)
            cell_res[part, tile] = jnp.where(live, fresh, cell_buf[part, tile])
        flush(0, part).start()
        flush(1, part).start()
        left = jnp.concatenate([patch_ref[row * LINE : row * LINE + DEEP, :] for row in range(ROWS)], axis=1)
        product = lax.dot_general(left, grad_ref[...], (((1,), (1,)), ((), ())), preferred_element_type=F32)
        if part:
            total_ref[...] += product
        elif last:
            total_ref[...] = acc_in_ref[...] + product
        else:
            total_ref[...] = product

    run((stages[12], stages[13]), (stages[14], stages[15]))


def compute(first, step, worker, carried, hidden, last):
    resident = pl.BlockSpec(memory_space=pltpu.VMEM)
    anywhere = pl.BlockSpec(memory_space=pl.ANY)
    operands = [worker] + carried
    scalars = pl.BlockSpec(memory_space=pltpu.SMEM)
    state = jax.ShapeDtypeStruct(hidden.shape, BF16)
    small = (TW, CIN, ROWS, COLS)
    medium = (TW, HID, ROWS, COLS)
    large = (2, TW, HID, ROWS, COLS)
    out_shape = [state, state]
    aliases = {}
    scratch = []
    if last:
        in_specs = [scalars] + [resident] * 10 + [anywhere] * 2
        aliases = {11: 0, 12: 1}
        out_shape.append(jax.ShapeDtypeStruct((GATES // (2 * ROWS), ROWS, DEEP), F32))
        out_shape.append(jax.ShapeDtypeStruct((GATES // (2 * ROWS), ROWS, DEEP), BF16))
    else:
        in_specs = [scalars] + [anywhere] * 4 + [resident] * 6
        out_shape.append(jax.ShapeDtypeStruct((DEEP, GATES), F32))
        out_shape.append(jax.ShapeDtypeStruct((GATES, DEEP), BF16))
        edge = (TW, KIN, COLS)
        out_shape += [jax.ShapeDtypeStruct(shape, BF16) for shape in (edge, edge, large, large)]
        scratch = [pltpu.VMEM(shape, BF16) for shape in (small, medium, large, large)]
        scratch += [pltpu.SemaphoreType.DMA((4, 2)), pltpu.SemaphoreType.DMA((2, 2))]
    stage = pltpu.VMEM((TW, HID * ROWS, COLS), F32)
    return pl.pallas_call(
        functools.partial(compute_kernel, first, step, last),
        in_specs=in_specs,
        out_specs=[anywhere, anywhere] + [resident] * (len(out_shape) - 2),
        scratch_shapes=scratch + [
            pltpu.VMEM(large, BF16),
            pltpu.VMEM(large, BF16),
            pltpu.SemaphoreType.DMA((2, 2)),
            pltpu.VMEM((DEEP, GATES), F32),
            pltpu.VMEM((GATES, ROW), F32),
            pltpu.VMEM((GATES, ROW), F32),
            *([pltpu.VMEM((TW, KIN * ROWS, COLS), F32), stage, stage, stage, stage, pltpu.VMEM((8, 128), F32)] * 2),
            pltpu.VMEM(((ROWS + 2) * LINE, ROW), BF16), pltpu.VMEM(((ROWS + 2) * LINE, ROW), BF16), pltpu.VMEM((GATES, ROWS * ROW), BF16), pltpu.VMEM((GATES, ROWS * ROW), BF16),
        ],
        out_shape=out_shape,
        input_output_aliases=aliases,
        compiler_params=pltpu.CompilerParams(vmem_limit_bytes=40 << 20),
        cost_estimate=pl.CostEstimate(
            flops=8 * TW * ROWS * COLS * TAPS * GATES, bytes_accessed=6 << 20, transcendentals=0
        ),
        name="second" if last else "first",
    )(*operands)


def shards(forcing, hidden_prev, cell_prev, hidden_grad, w_gates, gate_bias, worker):
    size = lax.axis_size("space")
    forcing, hidden, cell, grad = [
        pltpu.with_memory_space_constraint(array[0], pltpu.HBM)
        for array in (forcing, hidden_prev, cell_prev, hidden_grad)
    ]
    near, far, ending_0, leading_3, forcing_vmem, hidden_vmem = edges(forcing, hidden)
    near_halo = lax.ppermute(near, "space", [(i, i ^ 1) for i in range(size)])
    far_pairs = [(i, i + 1) for i in range(1, size - 1, 2)]
    far_halo = lax.ppermute(far, "space", far_pairs + [(j, i) for i, j in far_pairs])
    tiles = worker[0]
    hidden_part, cell_part, total, w, leading_1, ending_2, *ahead = compute(
        1, 1, tiles,
        [forcing, hidden, cell, grad, forcing_vmem, hidden_vmem, ending_0, leading_3, w_gates.T, gate_bias[None, :]],
        hidden, False,
    )
    hidden_next, cell_next, own, other = compute(
        0, 3, tiles,
        [forcing_vmem, hidden_vmem, *ahead, near_halo, leading_1, ending_2, far_halo, w, total, hidden_part, cell_part], hidden, True,
    )
    half = own + lax.ppermute(other, "space", [(i, i ^ 1) for i in range(size)]).astype(F32)
    groups = [list(range(core, size, 2)) for core in range(2)]
    pieces = lax.all_to_all(half.astype(BF16), "space", 0, 0, tiled=True, axis_index_groups=groups)
    mine = jnp.sum(pieces.astype(F32), axis=0).astype(BF16)
    years = lax.axis_size("dp")
    total = mine.astype(F32)
    for k in range(1, years):
        other = lax.ppermute(mine, "dp", [(i, (i + k) % years) for i in range(years)])
        total = total + other.astype(F32)
    return hidden_next[None], cell_next[None], total[:, :TAPS], total[:, TAPS]


def solution(mesh):
    tiles = P("dp", "space", None, None, None)
    return jax.shard_map(
        shards,
        mesh=mesh,
        in_specs=(tiles, tiles, tiles, tiles, P(), P(), P("dp", None)),
        out_specs=(tiles, tiles, P("space", None), P("space")),
        check_vma=False,
    )
```

time: 58.1 us -> 56.1 us (0.966)
  Pallas kernels: 26.7 us -> 24.7 us
    pallas_call x3, Pallas kernels: 26.7 us -> 24.7 us  [the longest x2 23.1 us: compute(): pl.pallas_call(functools.partial(compute_kernel, first, step, last), in_s...]
  transfers between devices with their start and end apart: 6 -> 6, of which waited for: 3 -> 3; matrix products, arithmetic and copies ran while one was open for 0% -> 0% of each run, Pallas kernels for 23% -> 22%
where the time goes in v3:
time: 56.1 us; the launch traced here: 55.9 us
  Pallas kernels  24.7 us (44%)
  blocking collectives  15.8 us (28%)
  starting transfers between devices  8.74 us (16%)
  waiting for transfers between devices  5.09 us (9%)
  between operations  0.76 us (1%)
  local copies, waits for them, and re-layouts  0.71 us (1%)
    pallas_call x2, Pallas kernels, compute(): pl.pallas_call(functools.partial(compute_kernel, first, step, last), in_s...  23.1 us
    all_to_all x1, blocking collectives, shards(): lax.all_to_all(half.astype(BF16), 'space', 0, 0, tiled=True, axis_index_g...  15.8 us
    ppermute x3, starting transfers between devices, shards(): lax.ppermute(mine, 'dp', [(i, (i + k) % years) for i in range(years)])  4.52 us
    ppermute x3, waiting for transfers between devices, shards(): lax.ppermute(mine, 'dp', [(i, (i + k) % years) for i in range(years)])  4.01 us
    ppermute x1, starting transfers between devices, shards(): lax.ppermute(other, 'space', [(i, i ^ 1) for i in range(size)]).astype(F32)  3.47 us
    pallas_call x1, Pallas kernels, edges(): pl.pallas_call(edge_kernel, in_specs=[pl.BlockSpec(memory_space=pl.ANY)]...  1.65 us
  transfers between devices with their start and end apart: 6, of which 3 were waited for; matrix products, arithmetic and copies ran while one was open for 0% of the time, Pallas kernels for 22%

profile of v3, /device:TPU:0, one launch (start us, length us, event | category | flops | bytes accessed | tf_op | source)
XLA Modules:
  0.0 55.9 jit_solution(6650612850203243836)
XLA Ops:
  0.6 0.0 copy-start.1
  0.6 0.0 copy-start.2
  0.7 0.0 copy-start
  0.7 1.7 %edges.1 = (bf16[4,80,128]{2,1,0:T(8,128)(2,1)S(1)}, bf16[4,80,128]{2,1,0:T(8,128)(2,1)S(1)}, bf16[4,80,128]{2,1,0:T(8,128)(2,1)S(1)}, bf16[4,80,128]{2,1,0:T(8,...) custom-call(bf16[16,16,8,128]{3,2,1,0:T(8,128)(2,1)} %bitcast.16, ...), custom_call_target="tpu_custom_call" | custom-call | bytes 3145728 | tf_op jit(solution)/shard_map/edges/pallas_call | solution.py:78
  2.3 0.1 collective-permute-start
  2.4 0.7 %collective-permute-start.1 = (bf16[4,80,128]{2,1,0:T(8,128)(2,1)S(1)}, bf16[4,80,128]{2,1,0:T(8,128)(2,1)S(1)}, u32[]{:S(2)}, u32[]{:S(2)}) collective-permute-start(bf16[4,80,128]{2,1,0:T(8,128)(2,1)S(1)} %get-tuple-element.31), channel_id=1, source_target_pairs={{4,8},{12,16},{20,24},{28,32},{36,40},{44,48},{52,56},{60,64},{68,... | collective-permute-start | bytes 245768 | tf_op jit(solution)/shard_map/ppermute | solution.py:368
  3.1 0.0 copy-done.1
  3.1 0.0 copy-done.2
  3.1 0.0 copy-done
  3.1 12.1 %first.1 = (bf16[16,64,8,128]{3,2,1,0:T(8,128)(2,1)}, bf16[16,64,8,128]{3,2,1,0:T(8,128)(2,1)}, f32[768,256]{1,0:T(8,128)S(1)}, bf16[256,768]{1,0:T(8,128)(2,1)S...) custom-call(s32[512]{0:T(512)S(1)} %bitcast.11, ...), custom_call_target="tpu_custom_call" | custom-call | flops 6039797760 | bytes 6291456 | tf_op jit(solution)/shard_map/first/pallas_call | solution.py:335
  15.2 0.0 collective-permute-done.rest_4_
  15.2 0.0 collective-permute-done.1.rest_7_
  15.2 11.0 %second.1 = (bf16[16,64,8,128]{3,2,1,0:T(8,128)(2,1)}, bf16[16,64,8,128]{3,2,1,0:T(8,128)(2,1)}, f32[16,8,768]{2,1,0:T(8,128)S(1)}, bf16[16,8,768]{2,1,0:T(8,128)(2,1)S(1)}) custom-call(s32[512]{0:T(512)S(1)} %bitcast.12, bf16[3,4,16,8,128]{4,3,2,1,0:T(8,128)(2,1)S(1)} %get-tuple-element.22.rest_4_.rest_0_, ...), custom_call_target="tpu_custom_call", output_to_operand_aliasing={{0}: (11, {}), {1}: (12, {})} | custom-call | flops 6039797760 | bytes 6291456 | tf_op jit(solution)/shard_map/second/pallas_call | solution.py:335
  26.2 3.5 %collective-permute-start.2 = (bf16[16,8,768]{2,1,0:T(8,128)(2,1)S(1)}, bf16[16,8,768]{2,1,0:T(8,128)(2,1)S(1)}, u32[]{:S(2)}, u32[]{:S(2)}) collective-permute-start(bf16[16,8,768]{2,1,0:T(8,128)(2,1)S(1)} %get-tuple-element.39), channel_id=1, source_target_pairs={{0,4},{4,0},{8,12},{12,8},{16,20},{20,16},{24,28},{28,24},{32,36},... | collective-permute-start | bytes 589832 | tf_op jit(solution)/shard_map/ppermute | solution.py:379
  29.7 1.1 %collective-permute-done.2 = bf16[16,8,768]{2,1,0:T(8,128)(2,1)S(1)} collective-permute-done((bf16[16,8,768]{2,1,0:T(8,128)(2,1)S(1)}, bf16[16,8,768]{2,1,0:T(8,128)(2,1)S(1)}, u32[]{:S(2)}, u32[]{:S(2)}) %collective-permute-start.2) | collective-permute-done | bytes 196640 | tf_op jit(solution)/shard_map/ppermute | solution.py:379
  30.8 15.8 %all_to_all.5 = bf16[16,8,768]{2,1,0:T(8,128)(2,1)S(1)} all-to-all(bf16[16,8,768]{2,1,0:T(8,128)(2,1)S(1)} %add_convert_fusion), channel_id=1, replica_groups={{0,8,16,24,32,40,48,56,64,72,80,88,96,104,112,120},{4,12,20,28,36,44,52..., dimensions={0} | all-to-all | bytes 393216 | tf_op jit(solution)/shard_map/all_to_all | solution.py:381
  46.6 2.8 %collective-permute-start.5 = (bf16[8,768]{1,0:T(8,128)(2,1)S(1)}, bf16[8,768]{1,0:T(8,128)(2,1)S(1)}, u32[]{:S(2)}, u32[]{:S(2)}) collective-permute-start(bf16[8,768]{1,0:T(8,128)(2,1)S(1)} %reduce_sum.12), channel_id=1, source_target_pairs={{0,3},{1,0},{2,1},{3,2},{4,7},{5,4},{6,5},{7,6},{8,11},{9,8},{10,9... | collective-permute-start | bytes 36872 | tf_op jit(solution)/shard_map/ppermute | solution.py:386
  49.4 0.8 %collective-permute-start.4 = (bf16[8,768]{1,0:T(8,128)(2,1)S(1)}, bf16[8,768]{1,0:T(8,128)(2,1)S(1)}, u32[]{:S(2)}, u32[]{:S(2)}) collective-permute-start(bf16[8,768]{1,0:T(8,128)(2,1)S(1)} %reduce_sum.12), channel_id=1, source_target_pairs={{0,2},{1,3},{2,0},{3,1},{4,6},{5,7},{6,4},{7,5},{8,10},{9,11},{10,... | collective-permute-start | bytes 36872 | tf_op jit(solution)/shard_map/ppermute | solution.py:386
  50.2 0.9 %collective-permute-start.3 = (bf16[8,768]{1,0:T(8,128)(2,1)S(1)}, bf16[8,768]{1,0:T(8,128)(2,1)S(1)}, u32[]{:S(2)}, u32[]{:S(2)}) collective-permute-start(bf16[8,768]{1,0:T(8,128)(2,1)S(1)} %reduce_sum.12), channel_id=1, source_target_pairs={{0,1},{1,2},{2,3},{3,0},{4,5},{5,6},{6,7},{7,4},{8,9},{9,10},{10,1... | collective-permute-start | bytes 36872 | tf_op jit(solution)/shard_map/ppermute | solution.py:386
  51.1 0.0 collective-permute-done.5
  51.1 3.5 %collective-permute-done.4 = bf16[8,768]{1,0:T(8,128)(2,1)S(1)} collective-permute-done((bf16[8,768]{1,0:T(8,128)(2,1)S(1)}, bf16[8,768]{1,0:T(8,128)(2,1)S(1)}, u32[]{:S(2)}, u32[]{:S(2)}) %collective-permute-start.4) | collective-permute-done | bytes 12320 | tf_op jit(solution)/shard_map/ppermute | solution.py:386
  54.6 0.5 collective-permute-done.3
  55.1 0.0 copy-start.3
  55.2 0.7 %slice_reduce_fusion = f32[8]{0:T(128)} fusion(f32[8,768]{1,0:T(8,128)S(1)} %convert_add_fusion), kind=kLoop, calls=%fused_computation.2 | loop fusion | bytes 64 | tf_op jit(solution)/shard_map/slice | solution.py:388
  (4 shorter events, 0.1 us)
Async XLA Ops:
  0.6 2.5 %copy-start.1 = (s32[1,512]{1,0:T(1,128)S(1)}, s32[1,512]{1,0:T(1,128)}, u32[]{:S(2)}) copy-start(s32[1,512]{1,0:T(1,128)} %param.13) | copy-start | bytes 6148
  0.6 2.5 %copy-start.2 = (f32[256]{0:T(256)S(1)}, f32[256]{0:T(256)}, u32[]{:S(2)}) copy-start(f32[256]{0:T(256)} %param.12) | copy-start | bytes 3076
  0.7 2.5 %copy-start = (bf16[256,720]{0,1:T(8,128)(2,1)S(1)}, bf16[256,720]{0,1:T(8,128)(2,1)}, u32[]{:S(2)}) copy-start(bf16[256,720]{0,1:T(8,128)(2,1)} %param.11) | copy-start | bytes 1105924
  2.3 12.9 %collective-permute-start = (bf16[4,80,128]{2,1,0:T(8,128)(2,1)S(1)}, bf16[4,80,128]{2,1,0:T(8,128)(2,1)S(1)}, u32[]{:S(2)}, u32[]{:S(2)}) collective-permute-start(bf16[4,80,128]{2,1,0:T(8,128)(2,1)S(1)} %get-tuple-element.28), channel_id=1, source_target_pairs={{0,4},{4,0},{8,12},{12,8},{16,20},{20,16},{24,28},{28,24},{32,36},... | collective-permute-start | bytes 245768 | tf_op jit(solution)/shard_map/ppermute | solution.py:366
  2.4 12.8 %collective-permute-start.1 = (bf16[4,80,128]{2,1,0:T(8,128)(2,1)S(1)}, bf16[4,80,128]{2,1,0:T(8,128)(2,1)S(1)}, u32[]{:S(2)}, u32[]{:S(2)}) collective-permute-start(bf16[4,80,128]{2,1,0:T(8,128)(2,1)S(1)} %get-tuple-element.31), channel_id=1, source_target_pairs={{4,8},{12,16},{20,24},{28,32},{36,40},{44,48},{52,56},{60,64},{68,... | collective-permute-start | bytes 245768 | tf_op jit(solution)/shard_map/ppermute | solution.py:368
  26.2 4.5 %collective-permute-start.2 = (bf16[16,8,768]{2,1,0:T(8,128)(2,1)S(1)}, bf16[16,8,768]{2,1,0:T(8,128)(2,1)S(1)}, u32[]{:S(2)}, u32[]{:S(2)}) collective-permute-start(bf16[16,8,768]{2,1,0:T(8,128)(2,1)S(1)} %get-tuple-element.39), channel_id=1, source_target_pairs={{0,4},{4,0},{8,12},{12,8},{16,20},{20,16},{24,28},{28,24},{32,36},... | collective-permute-start | bytes 589832 | tf_op jit(solution)/shard_map/ppermute | solution.py:379
  46.6 4.5 %collective-permute-start.5 = (bf16[8,768]{1,0:T(8,128)(2,1)S(1)}, bf16[8,768]{1,0:T(8,128)(2,1)S(1)}, u32[]{:S(2)}, u32[]{:S(2)}) collective-permute-start(bf16[8,768]{1,0:T(8,128)(2,1)S(1)} %reduce_sum.12), channel_id=1, source_target_pairs={{0,3},{1,0},{2,1},{3,2},{4,7},{5,4},{6,5},{7,6},{8,11},{9,8},{10,9... | collective-permute-start | bytes 36872 | tf_op jit(solution)/shard_map/ppermute | solution.py:386
  49.4 5.2 %collective-permute-start.4 = (bf16[8,768]{1,0:T(8,128)(2,1)S(1)}, bf16[8,768]{1,0:T(8,128)(2,1)S(1)}, u32[]{:S(2)}, u32[]{:S(2)}) collective-permute-start(bf16[8,768]{1,0:T(8,128)(2,1)S(1)} %reduce_sum.12), channel_id=1, source_target_pairs={{0,2},{1,3},{2,0},{3,1},{4,6},{5,7},{6,4},{7,5},{8,10},{9,11},{10,... | collective-permute-start | bytes 36872 | tf_op jit(solution)/shard_map/ppermute | solution.py:386
  50.2 4.9 %collective-permute-start.3 = (bf16[8,768]{1,0:T(8,128)(2,1)S(1)}, bf16[8,768]{1,0:T(8,128)(2,1)S(1)}, u32[]{:S(2)}, u32[]{:S(2)}) collective-permute-start(bf16[8,768]{1,0:T(8,128)(2,1)S(1)} %reduce_sum.12), channel_id=1, source_target_pairs={{0,1},{1,2},{2,3},{3,0},{4,5},{5,6},{6,7},{7,4},{8,9},{9,10},{10,1... | collective-permute-start | bytes 36872 | tf_op jit(solution)/shard_map/ppermute | solution.py:386
  55.1 0.7 %copy-start.3 = (f32[8,768]{1,0:T(8,128)}, f32[8,768]{1,0:T(8,128)S(1)}, u32[]{:S(2)}) copy-start(f32[8,768]{1,0:T(8,128)S(1)} %convert_add_fusion) | copy-start | bytes 73732

commit v4 on v3

--- a/solution.py
+++ b/solution.py
@@ -18,6 +18,8 @@
 WIDE = 3 * KIN
 LINE = 256
 CHUNK = 16
+WHOLE = (0, ROWS)
+SINGLE = tuple(range(ROWS + 1))
 TAPS = 3 * WIDE
 DEEP = 3 * LINE
 ROW = TW * COLS
@@ -186,8 +188,10 @@
             fill_ones(patch_ref)
         if not last:
             prepare(weight_ref, bias_ref, w_ref, total_ref)
+        waiting = []
         for part in range(2):
-            one_part(part, patches, grads[part], stages[0], *stages[6 * part : 6 * part + 6])
+            one_part(part, patches, grads, waiting, stages[0], *stages[6 * part : 6 * part + 6])
+        backward(waiting, patches, grads)
         if last:
             packed = jnp.concatenate(
                 [total_ref[tap * LINE : tap * LINE + WIDE, :] for tap in range(3)]
@@ -209,8 +213,24 @@
             for which in range(2):
                 flush(which, index).wait()
 
-    def one_part(part, patches, grad_ref, joined_0, joined_ref, before_ref, up_ref, hidden_new, cell_new, _):
-        patch_ref = patches[part]
+    def backward(waiting, patches, grads):
+        if not waiting:
+            return
+        part, start, stop = waiting.pop()
+        rows = range(start, stop)
+        left = jnp.concatenate([patches[part][row * LINE : row * LINE + DEEP, :] for row in rows], axis=1)
+        right = grads[part][:, start * ROW : stop * ROW]
+        product = lax.dot_general(left, right, (((1,), (1,)), ((), ())), preferred_element_type=F32)
+        if part or start:
+            total_ref[...] += product
+        elif last:
+            total_ref[...] = acc_in_ref[...] + product
+        else:
+            total_ref[...] = product
+
+    def one_part(part, patches, grads, waiting, joined_0, joined_ref, before_ref, up_ref, hidden_new, cell_new, _):
+        patch_ref, grad_ref = patches[part], grads[part]
+        cuts = SINGLE if last else WHOLE
         base = home * (BAND * TW) + (first + part * step) * TW
         forcing_buf, hidden_buf = state_of[part]
         lane = lax.broadcasted_iota(jnp.int32, (KIN, COLS), 1)
@@ -258,14 +278,16 @@
         for line in range(1, 3):
             build(line)
         forward(0)
-        if not last:
-            fetch(2, part).wait()
-            fetch(3, part).wait()
-        for tile in range(TW):
-            before_ref[tile] = cell_buf[part, tile].astype(F32).reshape(HID * ROWS, COLS)
-            live = worker_ref[base + tile] >= 0
-            up = grad_buf[part, tile].astype(F32).reshape(HID * ROWS, COLS)
-            up_ref[tile] = jnp.where(live, up, 0.0)
+        def state_rows():
+            if not last:
+                fetch(2, part).wait()
+                fetch(3, part).wait()
+            for tile in range(TW):
+                before_ref[tile] = cell_buf[part, tile].astype(F32).reshape(HID * ROWS, COLS)
+                live = worker_ref[base + tile] >= 0
+                up = grad_buf[part, tile].astype(F32).reshape(HID * ROWS, COLS)
+                up_ref[tile] = jnp.where(live, up, 0.0)
+
         for row in range(ROWS):
             if not last and row == 1 and part == 0:
                 fetch(2, 1).start()
@@ -284,7 +306,13 @@
             if row + 1 < ROWS:
                 build(row + 3)
                 forward(row + 1)
+            if row == 0:
+                state_rows()
+            backward(waiting, patches, grads)
             gates_of_row(pres[row % 2], before_ref, up_ref, hidden_new, cell_new, grad_ref, row)
+            for start, stop in zip(cuts, cuts[1:]):
+                if row + 1 == stop:
+                    waiting.append((part, start, stop))
 
         for tile in range(TW):
             live = worker_ref[base + tile] >= 0
@@ -294,14 +322,8 @@
             cell_res[part, tile] = jnp.where(live, fresh, cell_buf[part, tile])
         flush(0, part).start()
         flush(1, part).start()
-        left = jnp.concatenate([patch_ref[row * LINE : row * LINE + DEEP, :] for row in range(ROWS)], axis=1)
-        product = lax.dot_general(left, grad_ref[...], (((1,), (1,)), ((), ())), preferred_element_type=F32)
-        if part:
-            total_ref[...] += product
-        elif last:
-            total_ref[...] = acc_in_ref[...] + product
-        else:
-            total_ref[...] = product
+        if not last:
+            backward(waiting, patches, grads)
 
     run((stages[12], stages[13]), (stages[14], stages[15]))
 
@@ -382,7 +404,7 @@
     mine = jnp.sum(pieces.astype(F32), axis=0).astype(BF16)
     years = lax.axis_size("dp")
     total = mine.astype(F32)
-    for k in range(1, years):
+    for k in [years // 2] + [k for k in range(1, years) if k != years // 2]:
         other = lax.ppermute(mine, "dp", [(i, (i + k) % years) for i in range(years)])
         total = total + other.astype(F32)
     return hidden_next[None], cell_next[None], total[:, :TAPS], total[:, TAPS]

time: 56.1 us -> 55.8 us (level)
  waiting for transfers between devices: 5.09 us -> 3.98 us
  starting transfers between devices: 8.74 us -> 9.33 us
    ppermute x3, waiting for transfers between devices: 4.01 us -> 2.91 us  [shards(): lax.ppermute(mine, 'dp', [(i, (i + k) % years) for i in range(years)])]
    ppermute x3, starting transfers between devices: 4.52 us -> 5.12 us  [shards(): lax.ppermute(mine, 'dp', [(i, (i + k) % years) for i in range(years)])]
where the time goes in v4:
time: 55.8 us; the launch traced here: 55.3 us
  Pallas kernels  24.6 us (44%)
  blocking collectives  15.8 us (28%)
  starting transfers between devices  9.33 us (17%)
  waiting for transfers between devices  3.98 us (7%)
  between operations  0.76 us (1%)
  local copies, waits for them, and re-layouts  0.71 us (1%)
    pallas_call x2, Pallas kernels, compute(): pl.pallas_call(functools.partial(compute_kernel, first, step, last), in_s...  23 us
    all_to_all x1, blocking collectives, shards(): lax.all_to_all(half.astype(BF16), 'space', 0, 0, tiled=True, axis_index_g...  15.8 us
    ppermute x3, starting transfers between devices, shards(): lax.ppermute(mine, 'dp', [(i, (i + k) % years) for i in range(years)])  5.12 us
    ppermute x1, starting transfers between devices, shards(): lax.ppermute(other, 'space', [(i, i ^ 1) for i in range(size)]).astype(F32)  3.46 us
    ppermute x3, waiting for transfers between devices, shards(): lax.ppermute(mine, 'dp', [(i, (i + k) % years) for i in range(years)])  2.91 us
    pallas_call x1, Pallas kernels, edges(): pl.pallas_call(edge_kernel, in_specs=[pl.BlockSpec(memory_space=pl.ANY)]...  1.65 us
  transfers between devices with their start and end apart: 6, of which 3 were waited for; matrix products, arithmetic and copies ran while one was open for 0% of the time, Pallas kernels for 22%

profile of v4, /device:TPU:0, one launch (start us, length us, event | category | flops | bytes accessed | tf_op | source)
XLA Modules:
  0.0 55.3 jit_solution(13919508804610273399)
XLA Ops:
  0.6 0.0 copy-start.1
  0.6 0.0 copy-start.2
  0.7 1.7 %edges.1 = (bf16[4,80,128]{2,1,0:T(8,128)(2,1)S(1)}, bf16[4,80,128]{2,1,0:T(8,128)(2,1)S(1)}, bf16[4,80,128]{2,1,0:T(8,128)(2,1)S(1)}, bf16[4,80,128]{2,1,0:T(8,...) custom-call(bf16[16,16,8,128]{3,2,1,0:T(8,128)(2,1)} %bitcast.16, ...), custom_call_target="tpu_custom_call" | custom-call | bytes 3145728 | tf_op jit(solution)/shard_map/edges/pallas_call | solution.py:80
  2.3 0.1 collective-permute-start
  2.4 0.7 %collective-permute-start.1 = (bf16[4,80,128]{2,1,0:T(8,128)(2,1)S(1)}, bf16[4,80,128]{2,1,0:T(8,128)(2,1)S(1)}, u32[]{:S(2)}, u32[]{:S(2)}) collective-permute-start(bf16[4,80,128]{2,1,0:T(8,128)(2,1)S(1)} %get-tuple-element.31), channel_id=1, source_target_pairs={{4,8},{12,16},{20,24},{28,32},{36,40},{44,48},{52,56},{60,64},{68,... | collective-permute-start | bytes 245768 | tf_op jit(solution)/shard_map/ppermute | solution.py:390
  3.1 0.0 copy-done.1
  3.1 0.0 copy-done.2
  3.1 0.0 copy-done
  3.1 12.3 %first.1 = (bf16[16,64,8,128]{3,2,1,0:T(8,128)(2,1)}, bf16[16,64,8,128]{3,2,1,0:T(8,128)(2,1)}, f32[768,256]{1,0:T(8,128)S(1)}, bf16[256,768]{1,0:T(8,128)(2,1)S...) custom-call(s32[512]{0:T(512)S(1)} %bitcast.11, ...), custom_call_target="tpu_custom_call" | custom-call | flops 6039797760 | bytes 6291456 | tf_op jit(solution)/shard_map/first/pallas_call | solution.py:357
  15.4 0.0 collective-permute-done.rest_4_
  15.4 0.0 collective-permute-done.1.rest_7_
  15.4 10.7 %second.1 = (bf16[16,64,8,128]{3,2,1,0:T(8,128)(2,1)}, bf16[16,64,8,128]{3,2,1,0:T(8,128)(2,1)}, f32[16,8,768]{2,1,0:T(8,128)S(1)}, bf16[16,8,768]{2,1,0:T(8,128)(2,1)S(1)}) custom-call(s32[512]{0:T(512)S(1)} %bitcast.12, bf16[3,4,16,8,128]{4,3,2,1,0:T(8,128)(2,1)S(1)} %get-tuple-element.22.rest_4_.rest_0_, ...), custom_call_target="tpu_custom_call", output_to_operand_aliasing={{0}: (11, {}), {1}: (12, {})} | custom-call | flops 6039797760 | bytes 6291456 | tf_op jit(solution)/shard_map/second/pallas_call | solution.py:357
  26.1 3.5 %collective-permute-start.2 = (bf16[16,8,768]{2,1,0:T(8,128)(2,1)S(1)}, bf16[16,8,768]{2,1,0:T(8,128)(2,1)S(1)}, u32[]{:S(2)}, u32[]{:S(2)}) collective-permute-start(bf16[16,8,768]{2,1,0:T(8,128)(2,1)S(1)} %get-tuple-element.39), channel_id=1, source_target_pairs={{0,4},{4,0},{8,12},{12,8},{16,20},{20,16},{24,28},{28,24},{32,36},... | collective-permute-start | bytes 589832 | tf_op jit(solution)/shard_map/ppermute | solution.py:401
  29.6 1.1 %collective-permute-done.2 = bf16[16,8,768]{2,1,0:T(8,128)(2,1)S(1)} collective-permute-done((bf16[16,8,768]{2,1,0:T(8,128)(2,1)S(1)}, bf16[16,8,768]{2,1,0:T(8,128)(2,1)S(1)}, u32[]{:S(2)}, u32[]{:S(2)}) %collective-permute-start.2) | collective-permute-done | bytes 196640 | tf_op jit(solution)/shard_map/ppermute | solution.py:401
  30.7 15.8 %all_to_all.5 = bf16[16,8,768]{2,1,0:T(8,128)(2,1)S(1)} all-to-all(bf16[16,8,768]{2,1,0:T(8,128)(2,1)S(1)} %add_convert_fusion), channel_id=1, replica_groups={{0,8,16,24,32,40,48,56,64,72,80,88,96,104,112,120},{4,12,20,28,36,44,52..., dimensions={0} | all-to-all | bytes 393216 | tf_op jit(solution)/shard_map/all_to_all | solution.py:403
  46.5 2.8 %collective-permute-start.5 = (bf16[8,768]{1,0:T(8,128)(2,1)S(1)}, bf16[8,768]{1,0:T(8,128)(2,1)S(1)}, u32[]{:S(2)}, u32[]{:S(2)}) collective-permute-start(bf16[8,768]{1,0:T(8,128)(2,1)S(1)} %reduce_sum.12), channel_id=1, source_target_pairs={{0,3},{1,0},{2,1},{3,2},{4,7},{5,4},{6,5},{7,6},{8,11},{9,8},{10,9... | collective-permute-start | bytes 36872 | tf_op jit(solution)/shard_map/ppermute | solution.py:408
  49.3 0.0 collective-permute-start.4
  49.4 2.3 %collective-permute-start.3 = (bf16[8,768]{1,0:T(8,128)(2,1)S(1)}, bf16[8,768]{1,0:T(8,128)(2,1)S(1)}, u32[]{:S(2)}, u32[]{:S(2)}) collective-permute-start(bf16[8,768]{1,0:T(8,128)(2,1)S(1)} %reduce_sum.12), channel_id=1, source_target_pairs={{0,2},{1,3},{2,0},{3,1},{4,6},{5,7},{6,4},{7,5},{8,10},{9,11},{10,... | collective-permute-start | bytes 36872 | tf_op jit(solution)/shard_map/ppermute | solution.py:408
  51.6 0.0 collective-permute-done.5
  51.6 2.6 %collective-permute-done.4 = bf16[8,768]{1,0:T(8,128)(2,1)S(1)} collective-permute-done((bf16[8,768]{1,0:T(8,128)(2,1)S(1)}, bf16[8,768]{1,0:T(8,128)(2,1)S(1)}, u32[]{:S(2)}, u32[]{:S(2)}) %collective-permute-start.4) | collective-permute-done | bytes 12320 | tf_op jit(solution)/shard_map/ppermute | solution.py:408
  54.3 0.3 collective-permute-done.3
  54.6 0.0 copy-start.3
  54.6 0.7 %slice_reduce_fusion = f32[8]{0:T(128)} fusion(f32[8,768]{1,0:T(8,128)S(1)} %convert_add_fusion), kind=kLoop, calls=%fused_computation.2 | loop fusion | bytes 64 | tf_op jit(solution)/shard_map/slice | solution.py:410
  55.3 0.0 copy-done.3
  (4 shorter events, 0.1 us)
Async XLA Ops:
  0.6 2.5 %copy-start.1 = (s32[1,512]{1,0:T(1,128)S(1)}, s32[1,512]{1,0:T(1,128)}, u32[]{:S(2)}) copy-start(s32[1,512]{1,0:T(1,128)} %param.13) | copy-start | bytes 6148
  0.6 2.5 %copy-start.2 = (f32[256]{0:T(256)S(1)}, f32[256]{0:T(256)}, u32[]{:S(2)}) copy-start(f32[256]{0:T(256)} %param.12) | copy-start | bytes 3076
  0.7 2.5 %copy-start = (bf16[256,720]{0,1:T(8,128)(2,1)S(1)}, bf16[256,720]{0,1:T(8,128)(2,1)}, u32[]{:S(2)}) copy-start(bf16[256,720]{0,1:T(8,128)(2,1)} %param.11) | copy-start | bytes 1105924
  2.3 13.1 %collective-permute-start = (bf16[4,80,128]{2,1,0:T(8,128)(2,1)S(1)}, bf16[4,80,128]{2,1,0:T(8,128)(2,1)S(1)}, u32[]{:S(2)}, u32[]{:S(2)}) collective-permute-start(bf16[4,80,128]{2,1,0:T(8,128)(2,1)S(1)} %get-tuple-element.28), channel_id=1, source_target_pairs={{0,4},{4,0},{8,12},{12,8},{16,20},{20,16},{24,28},{28,24},{32,36},... | collective-permute-start | bytes 245768 | tf_op jit(solution)/shard_map/ppermute | solution.py:388
  2.4 13.0 %collective-permute-start.1 = (bf16[4,80,128]{2,1,0:T(8,128)(2,1)S(1)}, bf16[4,80,128]{2,1,0:T(8,128)(2,1)S(1)}, u32[]{:S(2)}, u32[]{:S(2)}) collective-permute-start(bf16[4,80,128]{2,1,0:T(8,128)(2,1)S(1)} %get-tuple-element.31), channel_id=1, source_target_pairs={{4,8},{12,16},{20,24},{28,32},{36,40},{44,48},{52,56},{60,64},{68,... | collective-permute-start | bytes 245768 | tf_op jit(solution)/shard_map/ppermute | solution.py:390
  26.1 4.5 %collective-permute-start.2 = (bf16[16,8,768]{2,1,0:T(8,128)(2,1)S(1)}, bf16[16,8,768]{2,1,0:T(8,128)(2,1)S(1)}, u32[]{:S(2)}, u32[]{:S(2)}) collective-permute-start(bf16[16,8,768]{2,1,0:T(8,128)(2,1)S(1)} %get-tuple-element.39), channel_id=1, source_target_pairs={{0,4},{4,0},{8,12},{12,8},{16,20},{20,16},{24,28},{28,24},{32,36},... | collective-permute-start | bytes 589832 | tf_op jit(solution)/shard_map/ppermute | solution.py:401
  46.5 5.1 %collective-permute-start.5 = (bf16[8,768]{1,0:T(8,128)(2,1)S(1)}, bf16[8,768]{1,0:T(8,128)(2,1)S(1)}, u32[]{:S(2)}, u32[]{:S(2)}) collective-permute-start(bf16[8,768]{1,0:T(8,128)(2,1)S(1)} %reduce_sum.12), channel_id=1, source_target_pairs={{0,3},{1,0},{2,1},{3,2},{4,7},{5,4},{6,5},{7,6},{8,11},{9,8},{10,9... | collective-permute-start | bytes 36872 | tf_op jit(solution)/shard_map/ppermute | solution.py:408
  49.3 4.9 %collective-permute-start.4 = (bf16[8,768]{1,0:T(8,128)(2,1)S(1)}, bf16[8,768]{1,0:T(8,128)(2,1)S(1)}, u32[]{:S(2)}, u32[]{:S(2)}) collective-permute-start(bf16[8,768]{1,0:T(8,128)(2,1)S(1)} %reduce_sum.12), channel_id=1, source_target_pairs={{0,1},{1,2},{2,3},{3,0},{4,5},{5,6},{6,7},{7,4},{8,9},{9,10},{10,1... | collective-permute-start | bytes 36872 | tf_op jit(solution)/shard_map/ppermute | solution.py:408
  49.4 5.2 %collective-permute-start.3 = (bf16[8,768]{1,0:T(8,128)(2,1)S(1)}, bf16[8,768]{1,0:T(8,128)(2,1)S(1)}, u32[]{:S(2)}, u32[]{:S(2)}) collective-permute-start(bf16[8,768]{1,0:T(8,128)(2,1)S(1)} %reduce_sum.12), channel_id=1, source_target_pairs={{0,2},{1,3},{2,0},{3,1},{4,6},{5,7},{6,4},{7,5},{8,10},{9,11},{10,... | collective-permute-start | bytes 36872 | tf_op jit(solution)/shard_map/ppermute | solution.py:408
  54.6 0.7 %copy-start.3 = (f32[8,768]{1,0:T(8,128)}, f32[8,768]{1,0:T(8,128)S(1)}, u32[]{:S(2)}) copy-start(f32[8,768]{1,0:T(8,128)S(1)} %convert_add_fusion) | copy-start | bytes 73732
